TPU v7x, 32 devices: a whole 2x2x4 slice. The times are simulated.
32 devices in a mesh: grp: 4 (over x, core), gx: 2 (over y), gy: 4 (over z).
Axes of the slice: x: 2, y: 2, z: 4, core: 2. Of those that a mesh axis runs over, the one named last changes fastest.
Arguments:
- pressure_start: float32 [16, 32, 512], P('gx', 'gy', 'grp'), may hold values from -6 to 6
- saturation: float32 [16, 32, 512], P('gx', 'gy', 'grp'), may hold values from 0.1 to 0.9
- permeability: float32 [16, 32, 512], P('gx', 'gy', 'grp'), may hold values from 0.1 to 10
- rock_type: int32 [16, 32, 512], P('gx', 'gy', 'grp'), may hold values from 0 to 3
- rock_table: float32 [5, 4], replicated, may hold values from 0.5 to 3
- well_cells: int32 [64], replicated, may hold values from 0 to 262143
- well_rates: float32 [64], replicated, may hold values from -12 to 12
- owner_map: int32 [2, 4, 4, 64, 1], P('gx', 'gy', 'grp'), may hold values from 0 to 1; in each aligned block of 64 rows (0 to 63, 64 to 127, ..., all dimensions but the last counted through in order) at most 64 rows name the same one
- stiffness: bfloat16 [2, 4, 4, 2, 64, 24, 24], P('gx', 'gy', 'grp'), may hold values from -0.008 to 0.2, as said below
- anchored: int32 [16, 32, 512], P('gx', 'gy', 'grp'), may hold values 0 or 1
Outputs:
- pressure: float32 [16, 32, 512], P('gx', 'gy', 'grp')
- vol_strain: float32 [16, 32, 512], P('gx', 'gy', 'grp')
Inputs may be any that keep to these rules, and one draw needn't show every extreme that they name: `owner_map`: of the 64 bricks of one device, at most 64 have the same owner. `stiffness`: the diagonal entries of every block lie between 0.1 and 0.2.
All inputs are finite; a program needn't handle non-finite values. No bound on the sum of `anchored` on one device may be relied on, other than what follows from the above.
Results may differ from a plain program's by a relative error of at most 0.0013.
Values may be sent and summed in bfloat16 or wider, within the bound.
A program may use at most 64 MiB of HBM per device.

v0:
```python
import jax
import jax.numpy as jnp
import numpy as np
from jax import lax
from jax.sharding import PartitionSpec as P

ITERS = 2
FLOW_PASSES = 4
MECH_PASSES = 3


OMEGA = 0.6
OFFSETS = tuple(
    ((along_x, along_y, along_z) for along_x in (0, 1) for along_y in (0, 1) for along_z in (0, 1))
)


def with_halo(cells, sides, width):
    for axis, dim in sides:
        count = lax.axis_size(axis)
        head = lax.slice_in_dim(cells, 0, width, axis=dim)
        tail = lax.slice_in_dim(cells, cells.shape[dim] - width, cells.shape[dim], axis=dim)
        cells = jnp.concatenate(
            [
                lax.ppermute(tail, axis, [(i, (i + 1) % count) for i in range(count)]),
                cells,
                lax.ppermute(head, axis, [((i + 1) % count, i) for i in range(count)]),
            ],
            axis=dim,
        )
    return cells


def corner_signs():
    sign_table = np.zeros((24,), np.float32)
    for comp_idx in range(3):
        for corner_idx, offset in enumerate(OFFSETS):
            sign_table[comp_idx * 8 + corner_idx] = 0.25 * (2 * offset[comp_idx] - 1)
    return jnp.asarray(sign_table)


def rock_values(rock_type, rock_table):
    rock_ids = jnp.arange(rock_table.shape[1], dtype=jnp.int32)
    one_hot = (rock_type[None] == rock_ids[:, None, None, None]).astype(jnp.float32)
    return jnp.tensordot(rock_table, one_hot, 1, precision=lax.Precision.HIGHEST)


def transmit(left_value, right_value):
    summed = left_value + right_value
    return 2.0 * left_value * right_value / jnp.where(summed > 0, summed, 1.0)


def neighbour_view(values, axis_dim, shift_by):
    starts = [1, 1, 1]
    starts[axis_dim] = 1 + shift_by
    finish = [
        starts[0] + values.shape[0] - 2,
        starts[1] + values.shape[1] - 2,
        starts[2] + values.shape[2] - 2,
    ]
    return lax.slice(values, starts, finish)


def relax_cells(padded_p, padded_k, numerator, denominator):
    centre = padded_k[1:-1, 1:-1, 1:-1]
    total_num = numerator
    total_den = denominator
    for axis_dim in range(3):
        for shift_by in (-1, 1):
            trans = transmit(centre, neighbour_view(padded_k, axis_dim, shift_by))
            total_num = total_num + trans * neighbour_view(padded_p, axis_dim, shift_by)
            total_den = total_den + trans
    return total_num / total_den


def trim_outside(extended, rim_width, index_now, axis_count, axis_dim):
    length = extended.shape[axis_dim]
    position = lax.broadcasted_iota(jnp.int32, extended.shape, axis_dim)
    outside = (position < rim_width) & (index_now == 0) | (position >= length - rim_width) & (
        index_now == axis_count - 1
    )
    return jnp.where(outside, 0.0, extended)


def trim_edges(extended, rim_width):
    extended = trim_outside(extended, rim_width, lax.axis_index("gy"), lax.axis_size("gy"), 2)
    return trim_outside(extended, rim_width, lax.axis_index("grp"), lax.axis_size("grp"), 3)


def flow_rim(stacked, rim_width):
    extended = with_halo(stacked, (("grp", 3), ("gx", 1), ("gy", 2)), rim_width)
    return trim_edges(extended, rim_width)


def shared_sum(partial_value):
    extended = with_halo(partial_value, (("grp", 3), ("gx", 1), ("gy", 2)), 1)
    extended = trim_edges(extended, 1)
    for axis_dim in (1, 2, 3):
        length = extended.shape[axis_dim]
        inner_part = lax.slice_in_dim(extended, 1, length - 1, axis=axis_dim)
        low_face = lax.slice_in_dim(extended, 0, 1, axis=axis_dim)
        high_face = lax.slice_in_dim(extended, length - 1, length, axis=axis_dim)
        low_pads = [(0, 0)] * 4
        high_pads = [(0, 0)] * 4
        low_pads[axis_dim] = (0, length - 3)
        high_pads[axis_dim] = (length - 3, 0)
        extended = inner_part + jnp.pad(low_face, low_pads) + jnp.pad(high_face, high_pads)
    return extended


def gather_corners(nodes):
    cells_x = nodes.shape[1] - 1
    cells_y = nodes.shape[2] - 1
    cells_z = nodes.shape[3] - 1
    pieces = [
        nodes[
            :,
            offset[0] : offset[0] + cells_x,
            offset[1] : offset[1] + cells_y,
            offset[2] : offset[2] + cells_z,
        ]
        for offset in OFFSETS
    ]
    stacked = jnp.stack(pieces, axis=1)
    return stacked.reshape((stacked.shape[0] * 8,) + stacked.shape[2:])


def spread_corners(element):
    comps = element.shape[0] // 8
    shaped = element.reshape((comps, 8) + element.shape[1:])
    summed = jnp.zeros((comps,) + tuple((extent + 1 for extent in element.shape[1:])), jnp.float32)
    for corner_idx, offset in enumerate(OFFSETS):
        pads = (
            (0, 0),
            (offset[0], 1 - offset[0]),
            (offset[1], 1 - offset[1]),
            (offset[2], 1 - offset[2]),
        )
        summed = summed + jnp.pad(shaped[:, corner_idx], pads)
    return summed


def per_device(
    pressure_start,
    saturation,
    permeability,
    rock_type,
    rock_table,
    well_cells,
    well_rates,
    owner_map,
    stiffness,
    anchored,
):
    cells_x, cells_y, cells_z = pressure_start.shape
    count_x = lax.axis_size("gx")
    total_y = cells_y * lax.axis_size("gy")
    total_z = cells_z * lax.axis_size("grp")
    start_x = lax.axis_index("gx") * cells_x
    start_y = lax.axis_index("gy") * cells_y
    start_z = lax.axis_index("grp") * cells_z
    rock_props = rock_values(rock_type, rock_table)
    mobility = jnp.exp(rock_props[0] * jnp.log(saturation)) + 2.0 * jnp.exp(
        rock_props[1] * jnp.log(1.0 - saturation)
    )
    conductance = permeability * mobility
    storage = rock_props[2]
    stress_term = rock_props[3]
    biot_coef = rock_props[4]
    plane_size = total_y * total_z
    well_x = well_cells // plane_size - start_x
    well_y = well_cells // total_z % total_y - start_y
    well_z = well_cells % total_z - start_z
    inside = (
        (well_x >= 0)
        & (well_x < cells_x)
        & (well_y >= 0)
        & (well_y < cells_y)
        & (well_z >= 0)
        & (well_z < cells_z)
    )
    local_flat = (well_x * cells_y + well_y) * cells_z + well_z
    cell_ids = jnp.arange(cells_x * cells_y * cells_z, dtype=jnp.int32)
    well_hits = ((local_flat[:, None] == cell_ids[None, :]) & inside[:, None]).astype(jnp.float32)
    source = jnp.dot(well_rates, well_hits, precision=lax.Precision.HIGHEST).reshape(
        cells_x, cells_y, cells_z
    )
    base_term = storage * pressure_start + source
    owners = owner_map.reshape(-1)
    capacity = stiffness.shape[4]
    one_hot = (owners[:, None] == jnp.arange(count_x, dtype=jnp.int32)[None, :]).astype(jnp.int32)
    before = jnp.cumsum(one_hot, axis=0) - one_hot
    brick_rank = jnp.sum(before * one_hot, axis=1)
    slot_index = owners * capacity + brick_rank
    held_blocks = stiffness.reshape(count_x, capacity, 24, 24)
    bricks = cells_x * cells_y
    fetched = lax.all_to_all(held_blocks, "gx", split_axis=0, concat_axis=0, tiled=True)
    brick_k = fetched.reshape(count_x * capacity, 24, 24)[slot_index]
    shaped = (
        jnp.diagonal(brick_k, axis1=1, axis2=2)
        .astype(jnp.float32)
        .reshape(cells_x, cells_y, 24)
        .transpose(2, 0, 1)
    )
    node_diag = shared_sum(
        spread_corners(jnp.broadcast_to(shaped[..., None], (24, cells_x, cells_y, cells_z)))
    )
    anchor_elem = jnp.broadcast_to(
        anchored.astype(jnp.float32)[None], (8, cells_x, cells_y, cells_z)
    )
    free_nodes = jnp.where(shared_sum(spread_corners(anchor_elem)) > 0, 0.0, 1.0).astype(
        jnp.float32
    )
    corner_sign = corner_signs()
    padded_k = flow_rim(conductance[None], 1)[0]
    displacement = jnp.zeros((3, cells_x + 1, cells_y + 1, cells_z + 1), jnp.float32)
    strain = jnp.zeros((cells_x, cells_y, cells_z), jnp.float32)
    pressure = pressure_start
    for outer_step in range(ITERS):
        numerator = base_term + stress_term * pressure - biot_coef * strain
        denominator = storage + stress_term
        for flow_step in range(FLOW_PASSES):
            pressure = relax_cells(flow_rim(pressure[None], 1)[0], padded_k, numerator, denominator)
        biot_load = (biot_coef * pressure)[None] * corner_sign[:, None, None, None]
        for mech_step in range(MECH_PASSES):
            corner_u = gather_corners(displacement)
            rounded = corner_u.astype(jnp.bfloat16)
            brick_u = rounded.transpose(1, 2, 0, 3).reshape(bricks, 24, cells_z)
            brick_force = jnp.einsum(
                "brk,bkz->brz", brick_k, brick_u, preferred_element_type=jnp.float32
            )
            element_force = brick_force.reshape(cells_x, cells_y, 24, cells_z).transpose(2, 0, 1, 3)
            residual = shared_sum(spread_corners(biot_load - element_force))
            displacement = free_nodes * (displacement + OMEGA * residual / node_diag)
        strain = jnp.tensordot(
            corner_sign, gather_corners(displacement), 1, precision=lax.Precision.HIGHEST
        )
    return (pressure, strain)


def solution(mesh):
    placed = (
        P("gx", "gy", "grp"),
        P("gx", "gy", "grp"),
        P("gx", "gy", "grp"),
        P("gx", "gy", "grp"),
        P(),
        P(),
        P(),
        P("gx", "gy", "grp", None, None),
        P("gx", "gy", "grp", None, None, None, None),
        P("gx", "gy", "grp"),
    )
    return jax.shard_map(
        per_device,
        mesh=mesh,
        in_specs=placed,
        out_specs=(P("gx", "gy", "grp"), P("gx", "gy", "grp")),
        check_vma=False,
    )
```

profile of v0, /device:TPU:0, one launch (start us, length us, event | category | flops | bytes accessed | tf_op | source)
XLA Modules:
  0.0 270.9 jit_solution(13648809386768754916)
XLA Ops:
  9.0 3.4 %all-to-all-start = ((bf16[2,2,18432]{2,1,0:T(2,128)(2,1)}), bf16[2,2,18432]{2,1,0:T(2,128)(2,1)S(1)}, u32[]{:S(2)}, u32[]{:S(2)}) async-start(bf16[2,2,18432]{2,1,0:T(2,128)(2,1)} %reshape.421), calls=%async_computation | async-start | bytes 294912 | tf_op jit(solution)/shard_map/all_to_all | solution.py:197
  25.3 3.8 %collective-permute-start.11 = (f32[1,10,1,130]{3,2,1,0:T(1,128)S(1)}, f32[1,10,1,130]{3,2,1,0:T(1,128)S(1)}, u32[]{:S(2)}, u32[]{:S(2)}) collective-permute-start(f32[1,10,1,130]{3,2,1,0:T(1,128)S(1)} %get-tuple-element.173), channel_id=1, source_target_pairs={{1,0},{2,1},{3,2},{0,3},{5,4},{6,5},{7,6},{4,7},{9,8},{10,9},{11,1... | collective-permute-start | bytes 15608 | tf_op jit(solution)/shard_map/ppermute | solution.py:27
  39.4 3.9 %collective-permute-start.17 = (f32[1,10,1,130]{3,2,1,0:T(1,128)S(1)}, f32[1,10,1,130]{3,2,1,0:T(1,128)S(1)}, u32[]{:S(2)}, u32[]{:S(2)}) collective-permute-start(f32[1,10,1,130]{3,2,1,0:T(1,128)S(1)} %get-tuple-element.169), channel_id=1, source_target_pairs={{1,0},{2,1},{3,2},{0,3},{5,4},{6,5},{7,6},{4,7},{9,8},{10,9},{11,1... | collective-permute-start | bytes 15608 | tf_op jit(solution)/shard_map/ppermute | solution.py:27
  48.0 2.8 %collective-permute-start.35 = (f32[1,11,1,131]{3,2,1,0:T(1,128)S(1)}, f32[1,11,1,131]{3,2,1,0:T(1,128)S(1)}, u32[]{:S(2)}, u32[]{:S(2)}) collective-permute-start(f32[1,11,1,131]{3,2,1,0:T(1,128)S(1)} %get-tuple-element.120), channel_id=1, source_target_pairs={{1,0},{2,1},{3,2},{0,3},{5,4},{6,5},{7,6},{4,7},{9,8},{10,9},{11,1... | collective-permute-start | bytes 17300 | tf_op jit(solution)/shard_map/ppermute | solution.py:27
  56.1 3.8 %collective-permute-start.23 = (f32[1,10,1,130]{3,2,1,0:T(1,128)S(1)}, f32[1,10,1,130]{3,2,1,0:T(1,128)S(1)}, u32[]{:S(2)}, u32[]{:S(2)}) collective-permute-start(f32[1,10,1,130]{3,2,1,0:T(1,128)S(1)} %get-tuple-element.167), channel_id=1, source_target_pairs={{1,0},{2,1},{3,2},{0,3},{5,4},{6,5},{7,6},{4,7},{9,8},{10,9},{11,1... | collective-permute-start | bytes 15608 | tf_op jit(solution)/shard_map/ppermute | solution.py:27
  69.8 3.9 %collective-permute-start.29 = (f32[1,10,1,130]{3,2,1,0:T(1,128)S(1)}, f32[1,10,1,130]{3,2,1,0:T(1,128)S(1)}, u32[]{:S(2)}, u32[]{:S(2)}) collective-permute-start(f32[1,10,1,130]{3,2,1,0:T(1,128)S(1)} %get-tuple-element.165), channel_id=1, source_target_pairs={{1,0},{2,1},{3,2},{0,3},{5,4},{6,5},{7,6},{4,7},{9,8},{10,9},{11,1... | collective-permute-start | bytes 15608 | tf_op jit(solution)/shard_map/ppermute | solution.py:27
  95.7 2.8 %collective-permute-start.41 = (f32[3,11,1,131]{3,2,1,0:T(1,128)S(1)}, f32[3,11,1,131]{3,2,1,0:T(1,128)S(1)}, u32[]{:S(2)}, u32[]{:S(2)}) collective-permute-start(f32[3,11,1,131]{3,2,1,0:T(1,128)S(1)} %get-tuple-element.42), channel_id=1, source_target_pairs={{1,0},{2,1},{3,2},{0,3},{5,4},{6,5},{7,6},{4,7},{9,8},{10,9},{11,1... | collective-permute-start | bytes 51884 | tf_op jit(solution)/shard_map/ppermute | solution.py:27
  99.3 3.4 %collective-permute-start.47 = (f32[3,11,1,131]{3,2,1,0:T(1,128)S(1)}, f32[3,11,1,131]{3,2,1,0:T(1,128)S(1)}, u32[]{:S(2)}, u32[]{:S(2)}) collective-permute-start(f32[3,11,1,131]{3,2,1,0:T(1,128)S(1)} %get-tuple-element.40), channel_id=1, source_target_pairs={{1,0},{2,1},{3,2},{0,3},{5,4},{6,5},{7,6},{4,7},{9,8},{10,9},{11,1... | collective-permute-start | bytes 51884 | tf_op jit(solution)/shard_map/ppermute | solution.py:27
  122.5 3.1 %collective-permute-start.53 = (f32[3,11,1,131]{3,2,1,0:T(1,128)S(1)}, f32[3,11,1,131]{3,2,1,0:T(1,128)S(1)}, u32[]{:S(2)}, u32[]{:S(2)}) collective-permute-start(f32[3,11,1,131]{3,2,1,0:T(1,128)S(1)} %get-tuple-element.38), channel_id=1, source_target_pairs={{1,0},{2,1},{3,2},{0,3},{5,4},{6,5},{7,6},{4,7},{9,8},{10,9},{11,1... | collective-permute-start | bytes 51884 | tf_op jit(solution)/shard_map/ppermute | solution.py:27
  133.3 3.1 %collective-permute-start.65 = (f32[1,10,1,130]{3,2,1,0:T(1,128)S(1)}, f32[1,10,1,130]{3,2,1,0:T(1,128)S(1)}, u32[]{:S(2)}, u32[]{:S(2)}) collective-permute-start(f32[1,10,1,130]{3,2,1,0:T(1,128)S(1)} %get-tuple-element.163), channel_id=1, source_target_pairs={{1,0},{2,1},{3,2},{0,3},{5,4},{6,5},{7,6},{4,7},{9,8},{10,9},{11,1... | collective-permute-start | bytes 15608 | tf_op jit(solution)/shard_map/ppermute | solution.py:27
  144.3 3.0 %collective-permute-start.59 = (f32[3,11,1,131]{3,2,1,0:T(1,128)S(1)}, f32[3,11,1,131]{3,2,1,0:T(1,128)S(1)}, u32[]{:S(2)}, u32[]{:S(2)}) collective-permute-start(f32[3,11,1,131]{3,2,1,0:T(1,128)S(1)} %get-tuple-element.36), channel_id=1, source_target_pairs={{1,0},{2,1},{3,2},{0,3},{5,4},{6,5},{7,6},{4,7},{9,8},{10,9},{11,1... | collective-permute-start | bytes 51884 | tf_op jit(solution)/shard_map/ppermute | solution.py:27
  161.0 10.4 %collective-permute-start.70 = (f32[1,10,1,130]{3,2,1,0:T(1,128)S(1)}, f32[1,10,1,130]{3,2,1,0:T(1,128)S(1)}, u32[]{:S(2)}, u32[]{:S(2)}) collective-permute-start(f32[1,10,1,130]{3,2,1,0:T(1,128)S(1)} %get-tuple-element.160), channel_id=1, source_target_pairs={{0,1},{1,2},{2,3},{3,0},{4,5},{5,6},{6,7},{7,4},{8,9},{9,10},{10,1... | collective-permute-start | bytes 15608 | tf_op jit(solution)/shard_map/ppermute | solution.py:25
  171.3 2.9 %collective-permute-start.71 = (f32[1,10,1,130]{3,2,1,0:T(1,128)S(1)}, f32[1,10,1,130]{3,2,1,0:T(1,128)S(1)}, u32[]{:S(2)}, u32[]{:S(2)}) collective-permute-start(f32[1,10,1,130]{3,2,1,0:T(1,128)S(1)} %get-tuple-element.161), channel_id=1, source_target_pairs={{1,0},{2,1},{3,2},{0,3},{5,4},{6,5},{7,6},{4,7},{9,8},{10,9},{11,1... | collective-permute-start | bytes 15608 | tf_op jit(solution)/shard_map/ppermute | solution.py:27
  185.3 2.7 %collective-permute-start.77 = (f32[1,10,1,130]{3,2,1,0:T(1,128)S(1)}, f32[1,10,1,130]{3,2,1,0:T(1,128)S(1)}, u32[]{:S(2)}, u32[]{:S(2)}) collective-permute-start(f32[1,10,1,130]{3,2,1,0:T(1,128)S(1)} %get-tuple-element.159), channel_id=1, source_target_pairs={{1,0},{2,1},{3,2},{0,3},{5,4},{6,5},{7,6},{4,7},{9,8},{10,9},{11,1... | collective-permute-start | bytes 15608 | tf_op jit(solution)/shard_map/ppermute | solution.py:27
  199.7 2.7 collective-permute-start.83
  207.3 4.1 %collective-permute-done.84 = f32[3,9,9,1]{3,2,1,0:T(8,128)S(1)} collective-permute-done((f32[3,9,9,1]{3,2,1,0:T(8,128)S(1)}, f32[3,9,9,1]{3,2,1,0:T(8,128)S(1)}, u32[]{:S(2)}, u32[]{:S(2)}) %collective-permute-start.84) | collective-permute-done | bytes 1004 | tf_op jit(solution)/shard_map/ppermute | solution.py:25
  214.6 2.6 collective-permute-done.86
  219.5 2.7 collective-permute-start.89
  228.8 3.8 %collective-permute-done.90 = f32[3,9,9,1]{3,2,1,0:T(8,128)S(1)} collective-permute-done((f32[3,9,9,1]{3,2,1,0:T(8,128)S(1)}, f32[3,9,9,1]{3,2,1,0:T(8,128)S(1)}, u32[]{:S(2)}, u32[]{:S(2)}) %collective-permute-start.90) | collective-permute-done | bytes 1004 | tf_op jit(solution)/shard_map/ppermute | solution.py:25
  236.4 2.6 collective-permute-done.92
  241.0 2.7 collective-permute-start.95
  250.3 3.6 %collective-permute-done.96 = f32[3,9,9,1]{3,2,1,0:T(8,128)S(1)} collective-permute-done((f32[3,9,9,1]{3,2,1,0:T(8,128)S(1)}, f32[3,9,9,1]{3,2,1,0:T(8,128)S(1)}, u32[]{:S(2)}, u32[]{:S(2)}) %collective-permute-start.96) | collective-permute-done | bytes 1004 | tf_op jit(solution)/shard_map/ppermute | solution.py:25
  258.1 2.6 collective-permute-done.98
  262.6 2.8 %collective-permute-start.101 = (f32[3,11,1,131]{3,2,1,0:T(1,128)S(1)}, f32[3,11,1,131]{3,2,1,0:T(1,128)S(1)}, u32[]{:S(2)}, u32[]{:S(2)}) collective-permute-start(f32[3,11,1,131]{3,2,1,0:T(1,128)S(1)} %get-tuple-element.30), channel_id=1, source_target_pairs={{1,0},{2,1},{3,2},{0,3},{5,4},{6,5},{7,6},{4,7},{9,8},{10,9},{11,1... | collective-permute-start | bytes 51884 | tf_op jit(solution)/shard_map/ppermute | solution.py:27
  (473 shorter events, 185.2 us)
Async XLA Ops:
  1.7 17.8 %collective-permute-start.30 = (f32[1,9,9,1]{3,2,1,0:T(8,128)S(1)}, f32[1,9,9,1]{3,2,1,0:T(8,128)S(1)}, u32[]{:S(2)}, u32[]{:S(2)}) collective-permute-start(f32[1,9,9,1]{3,2,1,0:T(8,128)S(1)} %get-tuple-element.128), channel_id=1, source_target_pairs={{0,8},{8,16},{16,24},{24,0},{1,9},{9,17},{17,25},{25,1},{2,10},{10... | collective-permute-start | bytes 980 | tf_op jit(solution)/shard_map/ppermute | solution.py:25
  2.2 17.4 %collective-permute-start.31 = (f32[1,9,9,1]{3,2,1,0:T(8,128)S(1)}, f32[1,9,9,1]{3,2,1,0:T(8,128)S(1)}, u32[]{:S(2)}, u32[]{:S(2)}) collective-permute-start(f32[1,9,9,1]{3,2,1,0:T(8,128)S(1)} %get-tuple-element.129), channel_id=1, source_target_pairs={{8,0},{16,8},{24,16},{0,24},{9,1},{17,9},{25,17},{1,25},{10,2},{18... | collective-permute-start | bytes 980 | tf_op jit(solution)/shard_map/ppermute | solution.py:27
  5.5 8.3 %collective-permute-start = (f32[1,8,8,1]{3,2,1,0:T(8,128)S(1)}, f32[1,8,8,1]{3,2,1,0:T(8,128)S(1)}, u32[]{:S(2)}, u32[]{:S(2)}) collective-permute-start(f32[1,8,8,1]{3,2,1,0:T(8,128)S(1)} %get-tuple-element.188), channel_id=1, source_target_pairs={{0,8},{8,16},{16,24},{24,0},{1,9},{9,17},{17,25},{25,1},{2,10},{10... | collective-permute-start | bytes 776 | tf_op jit(solution)/shard_map/ppermute | solution.py:25
  6.2 8.9 %collective-permute-start.1 = (f32[1,8,8,1]{3,2,1,0:T(8,128)S(1)}, f32[1,8,8,1]{3,2,1,0:T(8,128)S(1)}, u32[]{:S(2)}, u32[]{:S(2)}) collective-permute-start(f32[1,8,8,1]{3,2,1,0:T(8,128)S(1)} %get-tuple-element.189), channel_id=1, source_target_pairs={{8,0},{16,8},{24,16},{0,24},{9,1},{17,9},{25,17},{1,25},{10,2},{18... | collective-permute-start | bytes 776 | tf_op jit(solution)/shard_map/ppermute | solution.py:27
  7.4 10.0 %collective-permute-start.6 = (f32[1,8,8,1]{3,2,1,0:T(8,128)S(1)}, f32[1,8,8,1]{3,2,1,0:T(8,128)S(1)}, u32[]{:S(2)}, u32[]{:S(2)}) collective-permute-start(f32[1,8,8,1]{3,2,1,0:T(8,128)S(1)} %get-tuple-element.190), channel_id=1, source_target_pairs={{0,8},{8,16},{16,24},{24,0},{1,9},{9,17},{17,25},{25,1},{2,10},{10... | collective-permute-start | bytes 776 | tf_op jit(solution)/shard_map/ppermute | solution.py:25
  9.0 66.5 %all-to-all-start = ((bf16[2,2,18432]{2,1,0:T(2,128)(2,1)}), bf16[2,2,18432]{2,1,0:T(2,128)(2,1)S(1)}, u32[]{:S(2)}, u32[]{:S(2)}) async-start(bf16[2,2,18432]{2,1,0:T(2,128)(2,1)} %reshape.421), calls=%async_computation | async-start | bytes 294912 | tf_op jit(solution)/shard_map/all_to_all | solution.py:197
  17.6 7.5 %collective-permute-start.8 = (f32[1,1,8,130]{3,2,1,0:T(8,128)S(1)}, f32[1,1,8,130]{3,2,1,0:T(8,128)S(1)}, u32[]{:S(2)}, u32[]{:S(2)}) collective-permute-start(f32[1,1,8,130]{3,2,1,0:T(8,128)S(1)} %get-tuple-element.154), channel_id=1, source_target_pairs={{0,4},{4,0},{1,5},{5,1},{2,6},{6,2},{3,7},{7,3},{8,12},{12,8},{9,1... | collective-permute-start | bytes 12488 | tf_op jit(solution)/shard_map/ppermute | solution.py:25
  21.2 8.1 %collective-permute-start.4 = (f32[1,10,1,130]{3,2,1,0:T(1,128)S(1)}, f32[1,10,1,130]{3,2,1,0:T(1,128)S(1)}, u32[]{:S(2)}, u32[]{:S(2)}) collective-permute-start(f32[1,10,1,130]{3,2,1,0:T(1,128)S(1)} %get-tuple-element.170), channel_id=1, source_target_pairs={{0,1},{1,2},{2,3},{3,0},{4,5},{5,6},{6,7},{7,4},{8,9},{9,10},{10,1... | collective-permute-start | bytes 15608 | tf_op jit(solution)/shard_map/ppermute | solution.py:25
  78.9 8.3 %collective-permute-start.36 = (f32[3,9,9,1]{3,2,1,0:T(8,128)}, f32[3,9,9,1]{3,2,1,0:T(8,128)S(1)}, u32[]{:S(2)}, u32[]{:S(2)}) collective-permute-start(f32[3,9,9,1]{3,2,1,0:T(8,128)} %get-tuple-element.117), channel_id=1, source_target_pairs={{0,8},{8,16},{16,24},{24,0},{1,9},{9,17},{17,25},{25,1},{2,10},{10... | collective-permute-start | bytes 2924 | tf_op jit(solution)/shard_map/ppermute | solution.py:25
  79.0 8.3 %collective-permute-start.37 = (f32[3,9,9,1]{3,2,1,0:T(8,128)}, f32[3,9,9,1]{3,2,1,0:T(8,128)S(1)}, u32[]{:S(2)}, u32[]{:S(2)}) collective-permute-start(f32[3,9,9,1]{3,2,1,0:T(8,128)} %get-tuple-element.118), channel_id=1, source_target_pairs={{8,0},{16,8},{24,16},{0,24},{9,1},{17,9},{25,17},{1,25},{10,2},{18... | collective-permute-start | bytes 2924 | tf_op jit(solution)/shard_map/ppermute | solution.py:27
  85.3 6.8 %collective-permute-start.43 = (f32[3,9,9,1]{3,2,1,0:T(8,128)S(1)}, f32[3,9,9,1]{3,2,1,0:T(8,128)S(1)}, u32[]{:S(2)}, u32[]{:S(2)}) collective-permute-start(f32[3,9,9,1]{3,2,1,0:T(8,128)S(1)} %get-tuple-element.116), channel_id=1, source_target_pairs={{8,0},{16,8},{24,16},{0,24},{9,1},{17,9},{25,17},{1,25},{10,2},{18... | collective-permute-start | bytes 2924 | tf_op jit(solution)/shard_map/ppermute | solution.py:27
  87.3 7.0 %collective-permute-start.38 = (f32[3,1,9,131]{3,2,1,0:T(8,128)S(1)}, f32[3,1,9,131]{3,2,1,0:T(8,128)S(1)}, u32[]{:S(2)}, u32[]{:S(2)}) collective-permute-start(f32[3,1,9,131]{3,2,1,0:T(8,128)S(1)} %get-tuple-element.55), channel_id=1, source_target_pairs={{0,4},{4,0},{1,5},{5,1},{2,6},{6,2},{3,7},{7,3},{8,12},{12,8},{9,1... | collective-permute-start | bytes 42452 | tf_op jit(solution)/shard_map/ppermute | solution.py:25
  94.6 8.2 %collective-permute-start.40 = (f32[3,11,1,131]{3,2,1,0:T(1,128)S(1)}, f32[3,11,1,131]{3,2,1,0:T(1,128)S(1)}, u32[]{:S(2)}, u32[]{:S(2)}) collective-permute-start(f32[3,11,1,131]{3,2,1,0:T(1,128)S(1)} %get-tuple-element.41), channel_id=1, source_target_pairs={{0,1},{1,2},{2,3},{3,0},{4,5},{5,6},{6,7},{7,4},{8,9},{9,10},{10,1... | collective-permute-start | bytes 51884 | tf_op jit(solution)/shard_map/ppermute | solution.py:25
  95.7 7.1 %collective-permute-start.41 = (f32[3,11,1,131]{3,2,1,0:T(1,128)S(1)}, f32[3,11,1,131]{3,2,1,0:T(1,128)S(1)}, u32[]{:S(2)}, u32[]{:S(2)}) collective-permute-start(f32[3,11,1,131]{3,2,1,0:T(1,128)S(1)} %get-tuple-element.42), channel_id=1, source_target_pairs={{1,0},{2,1},{3,2},{0,3},{5,4},{6,5},{7,6},{4,7},{9,8},{10,9},{11,1... | collective-permute-start | bytes 51884 | tf_op jit(solution)/shard_map/ppermute | solution.py:27
  108.6 7.3 %collective-permute-start.49 = (f32[3,9,9,1]{3,2,1,0:T(8,128)S(1)}, f32[3,9,9,1]{3,2,1,0:T(8,128)S(1)}, u32[]{:S(2)}, u32[]{:S(2)}) collective-permute-start(f32[3,9,9,1]{3,2,1,0:T(8,128)S(1)} %get-tuple-element.114), channel_id=1, source_target_pairs={{8,0},{16,8},{24,16},{0,24},{9,1},{17,9},{25,17},{1,25},{10,2},{18... | collective-permute-start | bytes 2924 | tf_op jit(solution)/shard_map/ppermute | solution.py:27
  110.4 7.7 %collective-permute-start.60 = (f32[1,8,8,1]{3,2,1,0:T(8,128)S(1)}, f32[1,8,8,1]{3,2,1,0:T(8,128)S(1)}, u32[]{:S(2)}, u32[]{:S(2)}) collective-permute-start(f32[1,8,8,1]{3,2,1,0:T(8,128)S(1)} %get-tuple-element.180), channel_id=1, source_target_pairs={{0,8},{8,16},{16,24},{24,0},{1,9},{9,17},{17,25},{25,1},{2,10},{10... | collective-permute-start | bytes 776 | tf_op jit(solution)/shard_map/ppermute | solution.py:25
  110.5 7.6 %collective-permute-start.61 = (f32[1,8,8,1]{3,2,1,0:T(8,128)S(1)}, f32[1,8,8,1]{3,2,1,0:T(8,128)S(1)}, u32[]{:S(2)}, u32[]{:S(2)}) collective-permute-start(f32[1,8,8,1]{3,2,1,0:T(8,128)S(1)} %get-tuple-element.181), channel_id=1, source_target_pairs={{8,0},{16,8},{24,16},{0,24},{9,1},{17,9},{25,17},{1,25},{10,2},{18... | collective-permute-start | bytes 776 | tf_op jit(solution)/shard_map/ppermute | solution.py:27
  118.2 7.4 %collective-permute-start.62 = (f32[1,1,8,130]{3,2,1,0:T(8,128)S(1)}, f32[1,1,8,130]{3,2,1,0:T(8,128)S(1)}, u32[]{:S(2)}, u32[]{:S(2)}) collective-permute-start(f32[1,1,8,130]{3,2,1,0:T(8,128)S(1)} %get-tuple-element.144), channel_id=1, source_target_pairs={{0,4},{4,0},{1,5},{5,1},{2,6},{6,2},{3,7},{7,3},{8,12},{12,8},{9,1... | collective-permute-start | bytes 12488 | tf_op jit(solution)/shard_map/ppermute | solution.py:25
  130.8 7.0 %collective-permute-start.55 = (f32[3,9,9,1]{3,2,1,0:T(8,128)S(1)}, f32[3,9,9,1]{3,2,1,0:T(8,128)S(1)}, u32[]{:S(2)}, u32[]{:S(2)}) collective-permute-start(f32[3,9,9,1]{3,2,1,0:T(8,128)S(1)} %get-tuple-element.112), channel_id=1, source_target_pairs={{8,0},{16,8},{24,16},{0,24},{9,1},{17,9},{25,17},{1,25},{10,2},{18... | collective-permute-start | bytes 2924 | tf_op jit(solution)/shard_map/ppermute | solution.py:27
  132.5 14.8 %collective-permute-start.64 = (f32[1,10,1,130]{3,2,1,0:T(1,128)S(1)}, f32[1,10,1,130]{3,2,1,0:T(1,128)S(1)}, u32[]{:S(2)}, u32[]{:S(2)}) collective-permute-start(f32[1,10,1,130]{3,2,1,0:T(1,128)S(1)} %get-tuple-element.162), channel_id=1, source_target_pairs={{0,1},{1,2},{2,3},{3,0},{4,5},{5,6},{6,7},{7,4},{8,9},{9,10},{10,1... | collective-permute-start | bytes 15608 | tf_op jit(solution)/shard_map/ppermute | solution.py:25
  133.3 14.0 %collective-permute-start.65 = (f32[1,10,1,130]{3,2,1,0:T(1,128)S(1)}, f32[1,10,1,130]{3,2,1,0:T(1,128)S(1)}, u32[]{:S(2)}, u32[]{:S(2)}) collective-permute-start(f32[1,10,1,130]{3,2,1,0:T(1,128)S(1)} %get-tuple-element.163), channel_id=1, source_target_pairs={{1,0},{2,1},{3,2},{0,3},{5,4},{6,5},{7,6},{4,7},{9,8},{10,9},{11,1... | collective-permute-start | bytes 15608 | tf_op jit(solution)/shard_map/ppermute | solution.py:27
  161.0 14.8 %collective-permute-start.70 = (f32[1,10,1,130]{3,2,1,0:T(1,128)S(1)}, f32[1,10,1,130]{3,2,1,0:T(1,128)S(1)}, u32[]{:S(2)}, u32[]{:S(2)}) collective-permute-start(f32[1,10,1,130]{3,2,1,0:T(1,128)S(1)} %get-tuple-element.160), channel_id=1, source_target_pairs={{0,1},{1,2},{2,3},{3,0},{4,5},{5,6},{6,7},{7,4},{8,9},{9,10},{10,1... | collective-permute-start | bytes 15608 | tf_op jit(solution)/shard_map/ppermute | solution.py:25
  227.1 7.1 %collective-permute-start.91 = (f32[3,9,9,1]{3,2,1,0:T(8,128)S(1)}, f32[3,9,9,1]{3,2,1,0:T(8,128)S(1)}, u32[]{:S(2)}, u32[]{:S(2)}) collective-permute-start(f32[3,9,9,1]{3,2,1,0:T(8,128)S(1)} %get-tuple-element.108), channel_id=1, source_target_pairs={{8,0},{16,8},{24,16},{0,24},{9,1},{17,9},{25,17},{1,25},{10,2},{18... | collective-permute-start | bytes 2924 | tf_op jit(solution)/shard_map/ppermute | solution.py:27
  248.6 7.4 %collective-permute-start.97 = (f32[3,9,9,1]{3,2,1,0:T(8,128)S(1)}, f32[3,9,9,1]{3,2,1,0:T(8,128)S(1)}, u32[]{:S(2)}, u32[]{:S(2)}) collective-permute-start(f32[3,9,9,1]{3,2,1,0:T(8,128)S(1)} %get-tuple-element.106), channel_id=1, source_target_pairs={{8,0},{16,8},{24,16},{0,24},{9,1},{17,9},{25,17},{1,25},{10,2},{18... | collective-permute-start | bytes 2924 | tf_op jit(solution)/shard_map/ppermute | solution.py:27
  (90 other events, 435.3 us)
where the time goes:
time: 274 us; the launch traced here: 271 us
  starting transfers between devices  146 us (53%)
  waiting for transfers between devices  82.6 us (30%)
  other arithmetic  18.4 us (7%)
  local copies, waits for them, and re-layouts  15.1 us (6%)
  matrix products  6.65 us (2%)
    ppermute x51, starting transfers between devices, with_halo(): lax.ppermute(head, axis, [((i + 1) % count, i) for i in range(count)])  95.7 us
    ppermute x51, waiting for transfers between devices, with_halo(): lax.ppermute(tail, axis, [(i, (i + 1) % count) for i in range(count)])  62.3 us
    ppermute x51, starting transfers between devices, with_halo(): lax.ppermute(tail, axis, [(i, (i + 1) % count) for i in range(count)])  46.4 us
    ppermute x51, waiting for transfers between devices, with_halo(): lax.ppermute(head, axis, [((i + 1) % count, i) for i in range(count)])  20.3 us
  transfers between devices with their start and end apart: 103, of which 52 were waited for; matrix products, arithmetic and copies ran while one was open for 5% of the time, Pallas kernels for 0%

commit v1 on v0

v1 whole, which is shorter than its diff:
```python
import functools

import jax
import jax.numpy as jnp
import numpy as np
from jax import lax
from jax.experimental import pallas as pl
from jax.experimental.pallas import tpu as pltpu
from jax.sharding import PartitionSpec as P

ITERS = 2
FLOW_PASSES = 4
MECH_PASSES = 3
OMEGA = 0.6
MESH = pl.DeviceIdType.MESH


def corner_maps(cells_y):
    rows = np.zeros((4, 8, 24), np.float32)
    lines = cells_y + 1
    cols = np.zeros((cells_y, 24, 2 * lines * 8), np.float32)
    for comp in range(3):
        for dx in (0, 1):
            for dy in (0, 1):
                for dz in (0, 1):
                    entry = 8 * comp + 4 * dx + 2 * dy + dz
                    rows[2 * dx + dy, 4 * dz + comp, entry] = 1.0
                    for k in range(cells_y):
                        cols[k, entry, dx * lines * 8 + (k + dy) * 8 + 4 * dz + comp] = 1.0
    return rows, cols


def brick_blocks(owner_map, stiffness, count_x, bricks):
    owners = owner_map.reshape(-1)
    capacity = stiffness.shape[4]
    one_hot = (owners[:, None] == jnp.arange(count_x, dtype=jnp.int32)[None, :]).astype(jnp.int32)
    before = jnp.cumsum(one_hot, axis=0) - one_hot
    brick_rank = jnp.sum(before * one_hot, axis=1)
    slot_index = owners * capacity + brick_rank
    held_blocks = stiffness.reshape(count_x, capacity, 24, 24)
    fetched = lax.all_to_all(held_blocks, "gx", split_axis=0, concat_axis=0, tiled=True)
    return fetched.reshape(count_x * capacity, 24, 24)[slot_index]


def kernel(
    axes,
    table_ref,
    cells_ref,
    rates_ref,
    p0_ref,
    sat_ref,
    perm_ref,
    rock_ref,
    anch_ref,
    big_ref,
    diag_ref,
    p_out,
    s_out,
    p,
    cond,
    base,
    stress,
    biot,
    numer,
    inv_den,
    trans,
    bload,
    strain,
    disp,
    res,
    load,
    free,
    gain,
    y_send,
    z_send,
    x_recv,
    y_recv,
    z_recv,
    nz_send,
    nx_recv,
    ny_recv,
    nz_recv,
    fs_sem,
    fr_sem,
    ns_sem,
    nr_sem,
):
    count_x, count_y, count_z = axes
    cx, cy, cz = p0_ref.shape
    gx, gy, gz = lax.axis_index("gx"), lax.axis_index("gy"), lax.axis_index("grp")
    x_lo, x_hi = lax.rem(gx + count_x - 1, count_x), lax.rem(gx + 1, count_x)
    y_lo, y_hi = lax.max(gy - 1, 0), lax.min(gy + 1, count_y - 1)
    z_lo, z_hi = lax.max(gz - 1, 0), lax.min(gz + 1, count_z - 1)
    has = {
        ("gx", 0): None,
        ("gx", 1): None,
        ("gy", 0): gy > 0,
        ("gy", 1): gy < count_y - 1,
        ("grp", 0): gz > 0,
        ("grp", 1): gz < count_z - 1,
    }
    peer = {
        ("gx", 0): x_lo,
        ("gx", 1): x_hi,
        ("gy", 0): y_lo,
        ("gy", 1): y_hi,
        ("grp", 0): z_lo,
        ("grp", 1): z_hi,
    }

    def when(key, act):
        if has[key] is None:
            act()
        else:
            pl.when(has[key])(act)

    y_recv[...] = jnp.zeros_like(y_recv)
    z_recv[...] = jnp.zeros_like(z_recv)
    ny_recv[...] = jnp.zeros_like(ny_recv)
    nz_recv[...] = jnp.zeros_like(nz_recv)
    barrier = pltpu.get_barrier_semaphore()
    for key in peer:
        when(
            key,
            lambda key=key: pl.semaphore_signal(
                barrier, inc=1, device_id={key[0]: peer[key]}, device_id_type=MESH
            ),
        )

    rock = rock_ref[...]

    def rock_row(row):
        value = jnp.full(rock.shape, table_ref[row, 0], jnp.float32)
        for kind in range(1, table_ref.shape[1]):
            value = jnp.where(rock == kind, table_ref[row, kind], value)
        return value

    sat = sat_ref[...]
    cond[...] = perm_ref[...] * (
        jnp.exp(rock_row(0) * jnp.log(sat)) + 2.0 * jnp.exp(rock_row(1) * jnp.log(1.0 - sat))
    )
    p[...] = p0_ref[...]

    peers = 2
    for test in has.values():
        if test is not None:
            peers = peers + test.astype(jnp.int32)
    pl.semaphore_wait(barrier, peers)

    lane2 = lax.broadcasted_iota(jnp.int32, (cy, cz), 1)

    def exchange(copies):
        for axis, side, copy in copies:
            when((axis, side), copy.start)
        return copies

    def finish(copies):
        for axis, side, copy in copies:
            when((axis, side), copy.wait_send)
            when((axis, 1 - side), copy.wait_recv)

    def remote(axis, side, src, dst, send_sem, recv_sem):
        return (
            axis,
            side,
            pltpu.make_async_remote_copy(
                src_ref=src,
                dst_ref=dst,
                send_sem=send_sem,
                recv_sem=recv_sem,
                device_id={axis: peer[(axis, side)]},
                device_id_type=MESH,
            ),
        )

    def face_start(field, slot):
        for i in range(cx):
            y_send[slot, 0, i : i + 1, :] = field[i, 0:1, :]
            y_send[slot, 1, i : i + 1, :] = field[i, cy - 1 : cy, :]
        packed = jnp.zeros((cy, cz), jnp.float32)
        for i in range(cx):
            plane = field[i]
            packed = jnp.where(lane2 == i, pltpu.roll(plane, i, 1) if i else plane, packed)
            packed = jnp.where(lane2 == cx + i, pltpu.roll(plane, cx + i + 1, 1), packed)
        z_send[slot] = packed
        copies = []
        for side in (0, 1):
            at = 1 - side
            copies.append(
                remote(
                    "grp", side, z_send.at[slot], z_recv.at[slot, at],
                    fs_sem.at[slot, side], fr_sem.at[slot, at],
                )
            )
            copies.append(
                remote(
                    "gy", side, y_send.at[slot, side], y_recv.at[slot, at],
                    fs_sem.at[slot, 2 + side], fr_sem.at[slot, 2 + at],
                )
            )
            copies.append(
                remote(
                    "gx", side, field.at[side * (cx - 1)], x_recv.at[slot, at],
                    fs_sem.at[slot, 4 + side], fr_sem.at[slot, 4 + at],
                )
            )
        return exchange(copies)

    lane3 = lax.broadcasted_iota(jnp.int32, (cx, cy, cz), 2)
    sub3 = lax.broadcasted_iota(jnp.int32, (cx, cy, cz), 1)

    def views(field, slot):
        value = field[...]
        z_left = z_recv[slot, 0]
        z_right = z_recv[slot, 1]
        from_left = jnp.stack([pltpu.roll(z_left, cz - cx - i, 1) for i in range(cx)])
        from_right = jnp.stack([pltpu.roll(z_right, cz - 1 - i, 1) for i in range(cx)])
        y_left = jnp.stack(
            [jnp.broadcast_to(y_recv[slot, 0, i : i + 1, :], (cy, cz)) for i in range(cx)]
        )
        y_right = jnp.stack(
            [jnp.broadcast_to(y_recv[slot, 1, i : i + 1, :], (cy, cz)) for i in range(cx)]
        )
        return (
            jnp.concatenate([x_recv[slot, 0][None], value[:-1]], axis=0),
            jnp.concatenate([value[1:], x_recv[slot, 1][None]], axis=0),
            jnp.where(sub3 == 0, y_left, pltpu.roll(value, 1, 1)),
            jnp.where(sub3 == cy - 1, y_right, pltpu.roll(value, cy - 1, 1)),
            jnp.where(lane3 == 0, from_left, pltpu.roll(value, 1, 2)),
            jnp.where(lane3 == cz - 1, from_right, pltpu.roll(value, cz - 1, 2)),
        )

    cond_copies = face_start(cond, 0)

    storage = rock_row(2)
    stress[...] = rock_row(3)
    biot[...] = rock_row(4)
    plane_size = cy * count_y * cz * count_z
    flat = (
        (lax.broadcasted_iota(jnp.int32, (cx, cy, cz), 0) + gx * cx) * plane_size
        + (sub3 + gy * cy) * (cz * count_z)
        + lane3
        + gz * cz
    )

    def add_well(well, source):
        return source + jnp.where(flat == cells_ref[well], rates_ref[well], 0.0)

    source = lax.fori_loop(
        0, cells_ref.shape[0], add_well, jnp.zeros((cx, cy, cz), jnp.float32)
    )
    base[...] = storage * p0_ref[...] + source

    row = lax.broadcasted_iota(jnp.int32, (8, cz), 0)
    lane = lax.broadcasted_iota(jnp.int32, (8, cz), 1)
    comp = lax.rem(row, 4)
    along_z = row >= 4
    signs = {}
    for dx in (0, 1):
        for dy in (0, 1):
            signs[dx, dy] = jnp.where(
                comp == 0,
                0.25 * (2 * dx - 1),
                jnp.where(
                    comp == 1,
                    0.25 * (2 * dy - 1),
                    jnp.where(comp == 2, jnp.where(along_z, 0.25, -0.25), 0.0),
                ),
            )

    def share(slot):
        first = jnp.zeros((8, cz), jnp.float32)
        second = jnp.zeros((8, cz), jnp.float32)
        for x in range(cx + 1):
            for y in range(cy + 1):
                n = x * (cy + 1) + y
                line = res[x, y]
                first = jnp.where(lane == n, pltpu.roll(line, n, 1) if n else line, first)
                second = jnp.where(lane == n, pltpu.roll(line, n + 1, 1), second)
        nz_send[slot] = jnp.where(along_z, second, first)
        finish(
            exchange(
                [
                    remote(
                        "grp", side, nz_send.at[slot], nz_recv.at[slot, 1 - side],
                        ns_sem.at[slot, side], nr_sem.at[slot, 1 - side],
                    )
                    for side in (0, 1)
                ]
            )
        )
        beside = pltpu.roll(jnp.where(along_z, nz_recv[slot, 0], nz_recv[slot, 1]), 4, 0)
        for x in range(cx + 1):
            for y in range(cy + 1):
                n = x * (cy + 1) + y
                line = res[x, y]
                swapped = pltpu.roll(line, 4, 0)
                low = jnp.where(
                    lane == 0, pltpu.roll(beside, cz - n, 1) if n else beside, pltpu.roll(swapped, 1, 1)
                )
                high = jnp.where(
                    lane == cz - 1, pltpu.roll(beside, cz - 1 - n, 1), pltpu.roll(swapped, cz - 1, 1)
                )
                res[x, y] = line + jnp.where(along_z, high, low)
        finish(
            exchange(
                [
                    remote(
                        "gy", side, res.at[:, side * cy], ny_recv.at[slot, 1 - side],
                        ns_sem.at[slot, 2 + side], nr_sem.at[slot, 2 + 1 - side],
                    )
                    for side in (0, 1)
                ]
            )
        )
        for x in range(cx + 1):
            res[x, 0] = res[x, 0] + ny_recv[slot, 0, x]
            res[x, cy] = res[x, cy] + ny_recv[slot, 1, x]
        finish(
            exchange(
                [
                    remote(
                        "gx", side, res.at[side * cx], nx_recv.at[slot, 1 - side],
                        ns_sem.at[slot, 4 + side], nr_sem.at[slot, 4 + 1 - side],
                    )
                    for side in (0, 1)
                ]
            )
        )
        res[0] = res[0] + nx_recv[slot, 0]
        res[cx] = res[cx] + nx_recv[slot, 1]

    for x in range(cx + 1):
        for y in range(cy + 1):
            total = jnp.zeros((8, cz), jnp.float32)
            for dx in (0, 1):
                for dy in (0, 1):
                    i, k = x - dx, y - dy
                    if 0 <= i < cx and 0 <= k < cy:
                        held = jnp.broadcast_to(
                            anch_ref[i, k : k + 1, :].astype(jnp.float32), (8, cz)
                        )
                        total = total + jnp.where(comp == 3, held, diag_ref[i, k, 2 * dx + dy])
            res[x, y] = total
    share(0)
    for x in range(cx + 1):
        for y in range(cy + 1):
            line = res[x, y]
            count = jnp.where(along_z, line[7:8, :], line[3:4, :])
            keep = jnp.where((count > 0) | (comp == 3), 0.0, 1.0)
            free[x, y] = keep
            gain[x, y] = keep * OMEGA / jnp.where(comp == 3, 1.0, line)
    disp[...] = jnp.zeros_like(disp)
    strain[...] = jnp.zeros_like(strain)

    finish(cond_copies)
    centre = cond[...]
    total_den = storage + stress[...]
    for at, other in enumerate(views(cond, 0)):
        link = 2.0 * centre * other / (centre + other)
        trans[at] = link
        total_den = total_den + link
    inv_den[...] = 1.0 / total_den

    def outer(step, carry):
        numer[...] = base[...] + stress[...] * p[...] - biot[...] * strain[...]

        def flow(turn, carry):
            slot = 1 + step * FLOW_PASSES + turn
            finish(face_start(p, slot))
            total = numer[...]
            for at, other in enumerate(views(p, slot)):
                total = total + trans[at] * other
            p[...] = total * inv_den[...]
            return carry

        lax.fori_loop(0, FLOW_PASSES, flow, 0)
        bload[...] = biot[...] * p[...]
        for x in range(cx + 1):
            for y in range(cy + 1):
                total = jnp.zeros((8, cz), jnp.float32)
                for dx in (0, 1):
                    for dy in (0, 1):
                        i, k = x - dx, y - dy
                        if 0 <= i < cx and 0 <= k < cy:
                            total = total + signs[dx, dy] * jnp.broadcast_to(
                                bload[i, k : k + 1, :], (8, cz)
                            )
                load[x, y] = total

        def mech(turn, carry):
            slot = 1 + step * MECH_PASSES + turn
            res[...] = load[...]
            for i in range(cx):
                pair = disp[i : i + 2].reshape(2 * (cy + 1) * 8, cz).astype(jnp.bfloat16)
                force = jnp.dot(big_ref[i], pair, preferred_element_type=jnp.float32)
                force = force.reshape(4, cy, 8, cz)
                res[i, 0:cy] = res[i, 0:cy] - force[0]
                res[i, 1 : cy + 1] = res[i, 1 : cy + 1] - force[1]
                res[i + 1, 0:cy] = res[i + 1, 0:cy] - force[2]
                res[i + 1, 1 : cy + 1] = res[i + 1, 1 : cy + 1] - force[3]
            share(slot)
            for x in range(cx + 1):
                disp[x] = free[x] * disp[x] + gain[x] * res[x]
            return carry

        lax.fori_loop(0, MECH_PASSES, mech, 0)
        for i in range(cx):
            for k in range(cy):
                total = jnp.zeros((8, cz), jnp.float32)
                for dx in (0, 1):
                    for dy in (0, 1):
                        total = total + signs[dx, dy] * disp[i + dx, k + dy]
                strain[i, k : k + 1, :] = jnp.sum(total, axis=0, keepdims=True)
        return carry

    lax.fori_loop(0, ITERS, outer, 0)
    p_out[...] = p[...]
    s_out[...] = strain[...]


def per_device(
    pressure_start,
    saturation,
    permeability,
    rock_type,
    rock_table,
    well_cells,
    well_rates,
    owner_map,
    stiffness,
    anchored,
):
    cx, cy, cz = pressure_start.shape
    axes = (lax.axis_size("gx"), lax.axis_size("gy"), lax.axis_size("grp"))
    brick_k = brick_blocks(owner_map, stiffness, axes[0], cx * cy)
    rows, cols = corner_maps(cy)
    rows_b, cols_b = jnp.asarray(rows, jnp.bfloat16), jnp.asarray(cols, jnp.bfloat16)
    shaped = brick_k.reshape(cx, cy, 24, 24)
    spread = jnp.einsum(
        "ikrs,ksc->ikrc", shaped, cols_b, preferred_element_type=jnp.float32
    ).astype(jnp.bfloat16)
    big = jnp.einsum(
        "qmr,ikrc->iqkmc", rows_b, spread, preferred_element_type=jnp.float32
    ).astype(jnp.bfloat16)
    big = big.reshape(cx, 4 * cy * 8, cols.shape[2])
    diag = jnp.einsum(
        "qmr,ikr->ikqm",
        rows_b,
        jnp.diagonal(shaped, axis1=2, axis2=3),
        preferred_element_type=jnp.float32,
    )
    diag = jnp.broadcast_to(diag[..., None], (cx, cy, 4, 8, cz))

    cell = (cx, cy, cz)
    line = (cx + 1, cy + 1, 8, cz)
    flows = 1 + ITERS * FLOW_PASSES
    shares = 1 + ITERS * MECH_PASSES
    f32 = jnp.float32
    vmem = pl.BlockSpec(memory_space=pltpu.VMEM)
    smem = pl.BlockSpec(memory_space=pltpu.SMEM)
    return pl.pallas_call(
        functools.partial(kernel, axes),
        out_shape=(jax.ShapeDtypeStruct(cell, f32), jax.ShapeDtypeStruct(cell, f32)),
        in_specs=[smem] * 3 + [vmem] * 7,
        out_specs=(vmem, vmem),
        scratch_shapes=[pltpu.VMEM(cell, f32)] * 7
        + [pltpu.VMEM((6,) + cell, f32)]
        + [pltpu.VMEM(cell, f32)] * 2
        + [pltpu.VMEM(line, f32)] * 5
        + [
            pltpu.VMEM((flows, 2, cx, cz), f32),
            pltpu.VMEM((flows, cy, cz), f32),
            pltpu.VMEM((flows, 2, cy, cz), f32),
            pltpu.VMEM((flows, 2, cx, cz), f32),
            pltpu.VMEM((flows, 2, cy, cz), f32),
            pltpu.VMEM((shares, 8, cz), f32),
            pltpu.VMEM((shares, 2, cy + 1, 8, cz), f32),
            pltpu.VMEM((shares, 2, cx + 1, 8, cz), f32),
            pltpu.VMEM((shares, 2, 8, cz), f32),
            pltpu.SemaphoreType.DMA((flows, 6)),
            pltpu.SemaphoreType.DMA((flows, 6)),
            pltpu.SemaphoreType.DMA((shares, 6)),
            pltpu.SemaphoreType.DMA((shares, 6)),
        ],
        compiler_params=pltpu.CompilerParams(collective_id=0, has_side_effects=True),
    )(
        rock_table,
        well_cells,
        well_rates,
        pressure_start,
        saturation,
        permeability,
        rock_type,
        anchored,
        big,
        diag,
    )


def solution(mesh):
    cells = P("gx", "gy", "grp")
    placed = (
        cells,
        cells,
        cells,
        cells,
        P(),
        P(),
        P(),
        P("gx", "gy", "grp", None, None),
        P("gx", "gy", "grp", None, None, None, None),
        cells,
    )
    return jax.shard_map(
        per_device, mesh=mesh, in_specs=placed, out_specs=(cells, cells), check_vma=False
    )
```

time: 274 us -> 112 us (0.41); the launches traced: 271 us -> 112 us
  starting transfers between devices: 146 us -> 4.26 us
  Pallas kernels: 0 us -> 91.4 us
  waiting for transfers between devices: 82.6 us -> 3.61 us
  other arithmetic: 18.4 us -> 0.37 us
  matrix products: 6.65 us -> 0.87 us
  local copies, waits for them, and re-layouts: 15.1 us -> 10.6 us
    ppermute x102 -> x0, starting transfers between devices: 142 us -> none  [the longest x51 95.7 us: with_halo(): lax.ppermute(head, axis, [((i + 1) % count, i) for i in range(count)])]
    pallas_call x0 -> x1, Pallas kernels: none -> 91.4 us  [per_device(): pl.pallas_call(functools.partial(kernel, axes), out_shape=(jax.ShapeDtype...]
    ppermute x102 -> x0, waiting for transfers between devices: 82.6 us -> none  [the longest x51 62.3 us: with_halo(): lax.ppermute(tail, axis, [(i, (i + 1) % count) for i in range(count)])]
    dot_general x10 -> x2, matrix products: 6.65 us -> 0.87 us  [the longest x1 0.67 us: per_device(): jnp.einsum('qmr,ikrc->iqkmc', rows_b, spread, preferred_element_type=jnp....]
    slice x60 -> x0, local copies, waits for them, and re-layouts: 5.37 us -> none  [the longest x9 2.3 us: spread_corners(): summed = summed + jnp.pad(shaped[:, corner_idx], pads)]
    add x23 -> x0, other arithmetic: 4.58 us -> none  [the longest x8 2.78 us: spread_corners(): summed = summed + jnp.pad(shaped[:, corner_idx], pads)]
    all_to_all x1, waiting for transfers between devices: 0.01 us -> 3.61 us  [brick_blocks(): lax.all_to_all(held_blocks, 'gx', split_axis=0, concat_axis=0, tiled=True)]
    slice x25 -> x0, other arithmetic: 3.27 us -> none  [with_halo(): lax.slice_in_dim(cells, cells.shape[dim] - width, cells.shape[dim], axis=...]
  transfers between devices with their start and end apart: 103 -> 1, of which waited for: 52 -> 1; matrix products, arithmetic and copies ran while one was open for 5% -> 1% of each run, Pallas kernels for 0% -> 0%
where the time goes in v1:
time: 112 us
  Pallas kernels  91.4 us (82%)
  local copies, waits for them, and re-layouts  10.6 us (9%)
  starting transfers between devices  4.26 us (4%)
  waiting for transfers between devices  3.61 us (3%)
    pallas_call x1, Pallas kernels, per_device(): pl.pallas_call(functools.partial(kernel, axes), out_shape=(jax.ShapeDtype...  91.4 us
    unnamed x18, local copies, waits for them, and re-layouts  5.57 us
    all_to_all x1, starting transfers between devices, brick_blocks(): lax.all_to_all(held_blocks, 'gx', split_axis=0, concat_axis=0, tiled=True)  4.26 us
    all_to_all x1, waiting for transfers between devices, brick_blocks(): lax.all_to_all(held_blocks, 'gx', split_axis=0, concat_axis=0, tiled=True)  3.61 us
  transfers between devices with their start and end apart: 1, of which 1 were waited for; matrix products, arithmetic and copies ran while one was open for 1% of the time, Pallas kernels for 0%

profile of v1, /device:TPU:0, one launch (start us, length us, event | category | flops | bytes accessed | tf_op | source)
XLA Modules:
  0.0 111.9 jit_solution(12546386214358317533)
XLA Ops:
  0.6 0.0 copy-start
  0.7 0.9 copy-done
  1.6 0.9 reshape.70
  2.6 4.3 %all-to-all-start = ((bf16[2,2,18432]{2,1,0:T(2,128)(2,1)}), bf16[2,2,18432]{2,1,0:T(2,128)(2,1)S(1)}, u32[]{:S(2)}, u32[]{:S(2)}) async-start(bf16[2,2,18432]{2,1,0:T(2,128)(2,1)} %reshape.70), calls=%async_computation | async-start | bytes 294912 | tf_op jit(solution)/shard_map/all_to_all | solution.py:41
  6.8 0.7 copy.28.table_ref
  7.5 0.1 fusion.4
  7.6 0.1 reduce_window_sum.11
  7.7 0.2 select_reduce_fusion
  7.9 3.6 %all-to-all-done = bf16[2,2,18432]{2,1,0:T(2,128)(2,1)S(1)} async-done(((bf16[2,2,18432]{2,1,0:T(2,128)(2,1)}), bf16[2,2,18432]{2,1,0:T(2,128)(2,1)S(1)}, u32[]{:S(2)}, u32[]{:S(2)}) %all-to-all-start) | async-done | bytes 147488 | tf_op jit(solution)/shard_map/all_to_all | solution.py:41
  11.5 0.2 reshape.71
  11.7 0.4 copy.32
  12.2 0.0 copy-start.1
  12.2 0.0 copy-start.2
  12.2 0.7 gather_fusion
  12.9 0.8 copy.25
  13.7 0.7 fusion
  14.4 0.0 copy-start.3
  14.4 1.1 copy.24
  15.5 0.7 gather_fusion.1
  16.2 0.2 fusion.2
  16.4 1.4 %broadcast_in_dim.6.diag_ref = f32[8,8,4,8,128]{4,3,2,1,0:T(8,128)} broadcast(f32[8,8,4,8]{3,2,1,0:T(4,128)S(1)} %copy.27), dimensions={0,1,2,3} | broadcast | bytes 1056768 | tf_op jit(solution)/shard_map/broadcast_in_dim | solution.py:453
  17.8 91.4 %shard_map.131 = (f32[8,8,128]{2,1,0:T(8,128)}, f32[8,8,128]{2,1,0:T(8,128)}) custom-call(f32[5,4]{1,0:T(8,128)} %copy.28.table_ref, s32[64]{0:T(128)} %cells_ref.1, f32[64]{0:T(128)} %rates_ref.1, f32[8,8,128]{2,1,0:T(8,128)} %p0_ref.1, f32[8,8,128]{2,1,0:T(8,128)} %sat_ref.1, f32[8,8,128]{2,1,0:T(8,128)} %perm_ref.1, s32[8,8,128]{2,1,0:T(8,128)} %rock_ref.1, ...), custom_call_target="tpu_custom_call" | custom-call | tf_op jit(solution)/shard_map/pallas_call | solution.py:462
  109.2 1.4 %copy.40 = f32[8,8,128]{2,1,0:T(8,128)} copy(f32[8,8,128]{2,1,0:T(8,128)} %get-tuple-element.4) | data formatting | bytes 65536
  110.5 1.4 %copy.41 = f32[8,8,128]{2,1,0:T(8,128)} copy(f32[8,8,128]{2,1,0:T(8,128)} %get-tuple-element.5) | data formatting | bytes 65536
  (12 shorter events, 0.1 us)
Async XLA Ops:
  0.6 1.0 copy-start
  0.6 6.2 %copy-start.5 = (f32[5,4]{0,1:T(4,128)S(1)}, f32[5,4]{0,1:T(4,128)}, u32[]{:S(2)}) copy-start(f32[5,4]{0,1:T(4,128)} %param.16) | copy-start | bytes 244
  0.7 6.8 %copy-start.4 = (s32[1,1,1,64,1]{3,4,2,1,0:T(1,128)S(1)}, s32[1,1,1,64,1]{3,4,2,1,0:T(1,128)}, u32[]{:S(2)}) copy-start(s32[1,1,1,64,1]{3,4,2,1,0:T(1,128)} %param.19) | copy-start | bytes 772
  2.6 8.9 %all-to-all-start = ((bf16[2,2,18432]{2,1,0:T(2,128)(2,1)}), bf16[2,2,18432]{2,1,0:T(2,128)(2,1)S(1)}, u32[]{:S(2)}, u32[]{:S(2)}) async-start(bf16[2,2,18432]{2,1,0:T(2,128)(2,1)} %reshape.70), calls=%async_computation | async-start | bytes 294912 | tf_op jit(solution)/shard_map/all_to_all | solution.py:41
  12.2 1.5 %copy-start.1 = (bf16[8,24,144,1]{2,1,0,3:T(8,128)(2,1)S(1)}, bf16[8,24,144,1]{2,1,0,3:T(8,128)(2,1)}, u32[]{:S(2)}) copy-start(bf16[8,24,144,1]{2,1,0,3:T(8,128)(2,1)} %constant.37) | copy-start | bytes 165892
  12.2 1.5 %copy-start.2 = (bf16[4,8,24,1,1]{2,1,0,4,3:T(8,128)(2,1)S(1)}, bf16[4,8,24,1,1]{2,1,0,4,3:T(8,128)(2,1)}, u32[]{:S(2)}) copy-start(bf16[4,8,24,1,1]{2,1,0,4,3:T(8,128)(2,1)} %constant.38) | copy-start | bytes 4612
  14.4 1.8 %copy-start.3 = (bf16[4,8,24,1]{2,1,0,3:T(8,128)(2,1)S(1)}, bf16[4,8,24,1]{2,1,0,3:T(8,128)(2,1)}, u32[]{:S(2)}) copy-start(bf16[4,8,24,1]{2,1,0,3:T(8,128)(2,1)} %constant.39) | copy-start | bytes 4612

commit v2 on v1

--- a/solution.py
+++ b/solution.py
@@ -79,6 +79,7 @@
     nz_send,
     nx_recv,
     ny_recv,
+    nc_recv,
     nz_recv,
     fs_sem,
     fr_sem,
@@ -114,18 +115,49 @@
         else:
             pl.when(has[key])(act)
 
+    def near(shift_y, shift_z):
+        tests = [
+            test
+            for test in (
+                {-1: has["gy", 0], 0: None, 1: has["gy", 1]}[shift_y],
+                {-1: has["grp", 0], 0: None, 1: has["grp", 1]}[shift_z],
+            )
+            if test is not None
+        ]
+        return functools.reduce(jnp.logical_and, tests) if tests else None
+
+    groups = {(sy, sz): near(sy, sz) for sz in (-1, 0, 1) for sy in (-1, 0, 1)}
+    at_x, at_y, at_z = (
+        {-1: x_lo, 0: gx, 1: x_hi},
+        {-1: y_lo, 0: gy, 1: y_hi},
+        {-1: z_lo, 0: gz, 1: z_hi},
+    )
+
+    def members(group):
+        return [(sx,) + group for sx in (-1, 0, 1) if (sx,) + group != (0, 0, 0)]
+
+    def guarded(test, act):
+        if test is None:
+            act()
+        else:
+            pl.when(test)(act)
+
+    def device(shift):
+        return {"gx": at_x[shift[0]], "gy": at_y[shift[1]], "grp": at_z[shift[2]]}
+
     y_recv[...] = jnp.zeros_like(y_recv)
     z_recv[...] = jnp.zeros_like(z_recv)
     ny_recv[...] = jnp.zeros_like(ny_recv)
+    nc_recv[...] = jnp.zeros_like(nc_recv)
     nz_recv[...] = jnp.zeros_like(nz_recv)
     barrier = pltpu.get_barrier_semaphore()
-    for key in peer:
-        when(
-            key,
-            lambda key=key: pl.semaphore_signal(
-                barrier, inc=1, device_id={key[0]: peer[key]}, device_id_type=MESH
-            ),
-        )
+
+    def greet(group):
+        for shift in members(group):
+            pl.semaphore_signal(barrier, inc=1, device_id=device(shift), device_id_type=MESH)
+
+    for group, test in groups.items():
+        guarded(test, lambda group=group: greet(group))
 
     rock = rock_ref[...]
 
@@ -141,11 +173,10 @@
     )
     p[...] = p0_ref[...]
 
-    peers = 2
-    for test in has.values():
-        if test is not None:
-            peers = peers + test.astype(jnp.int32)
-    pl.semaphore_wait(barrier, peers)
+    def span(axis):
+        return 1 + has[axis, 0].astype(jnp.int32) + has[axis, 1].astype(jnp.int32)
+
+    pl.semaphore_wait(barrier, 3 * span("gy") * span("grp") - 1)
 
     lane2 = lax.broadcasted_iota(jnp.int32, (cy, cz), 1)
 
@@ -231,6 +262,7 @@
         )
 
     cond_copies = face_start(cond, 0)
+    first_copies = face_start(p, 1)
 
     storage = rock_row(2)
     stress[...] = rock_row(3)
@@ -268,7 +300,40 @@
                 ),
             )
 
-    def share(slot):
+    edge = lane == jnp.where(along_z, cz - 1, 0)
+    across = lax.rem(lane, cy + 1)
+    line_x = {
+        -1: lane <= cy,
+        0: None,
+        1: (lane >= cx * (cy + 1)) & (lane < (cx + 1) * (cy + 1)),
+    }
+    line_y = {-1: across == 0, 0: None, 1: across == cy}
+
+    def message(slot, shift):
+        sx, sy, sz = shift
+        code = 9 * (sz + 1) + 3 * (sy + 1) + sx + 1
+        if sz:
+            src = nz_send.at[slot]
+            dst = nz_recv.at[slot, z_place(-sx, -sy, -sz)]
+        elif sx and sy:
+            src = res.at[(sx + 1) // 2 * cx, (sy + 1) // 2 * cy]
+            dst = nc_recv.at[slot, (1 - sx) + (1 - sy) // 2]
+        elif sx:
+            src = res.at[(sx + 1) // 2 * cx]
+            dst = nx_recv.at[slot, (1 - sx) // 2]
+        else:
+            src = res.at[:, (sy + 1) // 2 * cy]
+            dst = ny_recv.at[slot, (1 - sy) // 2]
+        return pltpu.make_async_remote_copy(
+            src_ref=src,
+            dst_ref=dst,
+            send_sem=ns_sem.at[slot, code],
+            recv_sem=nr_sem.at[slot, 26 - code],
+            device_id=device(shift),
+            device_id_type=MESH,
+        )
+
+    def share_start(slot):
         first = jnp.zeros((8, cz), jnp.float32)
         second = jnp.zeros((8, cz), jnp.float32)
         for x in range(cx + 1):
@@ -277,58 +342,61 @@
                 line = res[x, y]
                 first = jnp.where(lane == n, pltpu.roll(line, n, 1) if n else line, first)
                 second = jnp.where(lane == n, pltpu.roll(line, n + 1, 1), second)
+                swapped = pltpu.roll(line, 4, 0)
+                moved = jnp.where(along_z, pltpu.roll(swapped, cz - 1, 1), pltpu.roll(swapped, 1, 1))
+                res[x, y] = line + jnp.where(edge, 0.0, moved)
         nz_send[slot] = jnp.where(along_z, second, first)
-        finish(
-            exchange(
-                [
-                    remote(
-                        "grp", side, nz_send.at[slot], nz_recv.at[slot, 1 - side],
-                        ns_sem.at[slot, side], nr_sem.at[slot, 1 - side],
-                    )
-                    for side in (0, 1)
-                ]
-            )
-        )
-        beside = pltpu.roll(jnp.where(along_z, nz_recv[slot, 0], nz_recv[slot, 1]), 4, 0)
-        for x in range(cx + 1):
-            for y in range(cy + 1):
-                n = x * (cy + 1) + y
-                line = res[x, y]
-                swapped = pltpu.roll(line, 4, 0)
-                low = jnp.where(
-                    lane == 0, pltpu.roll(beside, cz - n, 1) if n else beside, pltpu.roll(swapped, 1, 1)
-                )
-                high = jnp.where(
-                    lane == cz - 1, pltpu.roll(beside, cz - 1 - n, 1), pltpu.roll(swapped, cz - 1, 1)
-                )
-                res[x, y] = line + jnp.where(along_z, high, low)
-        finish(
-            exchange(
-                [
-                    remote(
-                        "gy", side, res.at[:, side * cy], ny_recv.at[slot, 1 - side],
-                        ns_sem.at[slot, 2 + side], nr_sem.at[slot, 2 + 1 - side],
-                    )
-                    for side in (0, 1)
-                ]
-            )
-        )
-        for x in range(cx + 1):
-            res[x, 0] = res[x, 0] + ny_recv[slot, 0, x]
-            res[x, cy] = res[x, cy] + ny_recv[slot, 1, x]
-        finish(
-            exchange(
-                [
-                    remote(
-                        "gx", side, res.at[side * cx], nx_recv.at[slot, 1 - side],
-                        ns_sem.at[slot, 4 + side], nr_sem.at[slot, 4 + 1 - side],
-                    )
-                    for side in (0, 1)
-                ]
-            )
-        )
-        res[0] = res[0] + nx_recv[slot, 0]
-        res[cx] = res[cx] + nx_recv[slot, 1]
+
+        def go(group):
+            for shift in members(group):
+                message(slot, shift).start()
+
+        for group, test in groups.items():
+            guarded(test, lambda group=group: go(group))
+
+    def share_arrive(slot):
+        def arrive(group):
+            for sx, sy, sz in members(group):
+                message(slot, (-sx, -sy, -sz)).wait_recv()
+
+        for group, test in groups.items():
+            guarded(test, lambda group=group: arrive(group))
+        sides = []
+        for sz in (-1, 1):
+            total = jnp.zeros((8, cz), jnp.float32)
+            for sx in (-1, 0, 1):
+                for sy in (-1, 0, 1):
+                    part = nz_recv[slot, z_place(sx, sy, sz)]
+                    turn = (sx * cx * (cy + 1) + sy * cy) % cz
+                    part = pltpu.roll(part, turn, 1) if turn else part
+                    for test in (line_x[sx], line_y[sy]):
+                        if test is not None:
+                            part = jnp.where(test, part, 0.0)
+                    total = total + part
+            sides.append(total)
+        return pltpu.roll(jnp.where(along_z, sides[0], sides[1]), 4, 0)
+
+    def z_place(sx, sy, sz):
+        return 9 * (sz + 1) // 2 + 3 * (sy + 1) + sx + 1
+
+    def share_line(slot, beside, x, y):
+        n = x * (cy + 1) + y
+        total = res[x, y] + jnp.where(edge, jnp.broadcast_to(beside[:, n : n + 1], (8, cz)), 0.0)
+        if x in (0, cx):
+            total = total + nx_recv[slot, x // cx, y]
+        if y in (0, cy):
+            total = total + ny_recv[slot, y // cy, x]
+        if x in (0, cx) and y in (0, cy):
+            total = total + nc_recv[slot, 2 * (x // cx) + y // cy]
+        return total
+
+    def share_end(slot):
+        def sent(group):
+            for shift in members(group):
+                message(slot, shift).wait_send()
+
+        for group, test in groups.items():
+            guarded(test, lambda group=group: sent(group))
 
     for x in range(cx + 1):
         for y in range(cy + 1):
@@ -342,14 +410,7 @@
                         )
                         total = total + jnp.where(comp == 3, held, diag_ref[i, k, 2 * dx + dy])
             res[x, y] = total
-    share(0)
-    for x in range(cx + 1):
-        for y in range(cy + 1):
-            line = res[x, y]
-            count = jnp.where(along_z, line[7:8, :], line[3:4, :])
-            keep = jnp.where((count > 0) | (comp == 3), 0.0, 1.0)
-            free[x, y] = keep
-            gain[x, y] = keep * OMEGA / jnp.where(comp == 3, 1.0, line)
+    share_start(0)
     disp[...] = jnp.zeros_like(disp)
     strain[...] = jnp.zeros_like(strain)
 
@@ -362,19 +423,44 @@
         total_den = total_den + link
     inv_den[...] = 1.0 / total_den
 
-    def outer(step, carry):
+    def relax(slot):
+        total = numer[...]
+        for at, other in enumerate(views(p, slot)):
+            total = total + trans[at] * other
+        p[...] = total * inv_den[...]
+
+    def settle(slot):
+        share_start(slot)
+        beside = share_arrive(slot)
+        for x in range(cx + 1):
+            for y in range(cy + 1):
+                total = share_line(slot, beside, x, y)
+                disp[x, y] = free[x, y] * disp[x, y] + gain[x, y] * total
+        share_end(slot)
+
+    for step in range(ITERS):
         numer[...] = base[...] + stress[...] * p[...] - biot[...] * strain[...]
 
         def flow(turn, carry):
             slot = 1 + step * FLOW_PASSES + turn
             finish(face_start(p, slot))
-            total = numer[...]
-            for at, other in enumerate(views(p, slot)):
-                total = total + trans[at] * other
-            p[...] = total * inv_den[...]
+            relax(slot)
             return carry
 
-        lax.fori_loop(0, FLOW_PASSES, flow, 0)
+        if step == 0:
+            finish(first_copies)
+            relax(1)
+        lax.fori_loop(1 if step == 0 else 0, FLOW_PASSES, flow, 0)
+        if step == 0:
+            beside = share_arrive(0)
+            for x in range(cx + 1):
+                for y in range(cy + 1):
+                    line = share_line(0, beside, x, y)
+                    count = jnp.where(along_z, line[7:8, :], line[3:4, :])
+                    keep = jnp.where((count > 0) | (comp == 3), 0.0, 1.0)
+                    free[x, y] = keep
+                    gain[x, y] = keep * OMEGA / jnp.where(comp == 3, 1.0, line)
+            share_end(0)
         bload[...] = biot[...] * p[...]
         for x in range(cx + 1):
             for y in range(cy + 1):
@@ -399,12 +485,13 @@
                 res[i, 1 : cy + 1] = res[i, 1 : cy + 1] - force[1]
                 res[i + 1, 0:cy] = res[i + 1, 0:cy] - force[2]
                 res[i + 1, 1 : cy + 1] = res[i + 1, 1 : cy + 1] - force[3]
-            share(slot)
-            for x in range(cx + 1):
-                disp[x] = free[x] * disp[x] + gain[x] * res[x]
+            settle(slot)
             return carry
 
-        lax.fori_loop(0, MECH_PASSES, mech, 0)
+        if step == 0:
+            res[...] = load[...]
+            settle(1)
+        lax.fori_loop(1 if step == 0 else 0, MECH_PASSES, mech, 0)
         for i in range(cx):
             for k in range(cy):
                 total = jnp.zeros((8, cz), jnp.float32)
@@ -412,9 +499,7 @@
                     for dy in (0, 1):
                         total = total + signs[dx, dy] * disp[i + dx, k + dy]
                 strain[i, k : k + 1, :] = jnp.sum(total, axis=0, keepdims=True)
-        return carry
-
-    lax.fori_loop(0, ITERS, outer, 0)
+
     p_out[...] = p[...]
     s_out[...] = strain[...]
 
@@ -477,11 +562,12 @@
             pltpu.VMEM((shares, 8, cz), f32),
             pltpu.VMEM((shares, 2, cy + 1, 8, cz), f32),
             pltpu.VMEM((shares, 2, cx + 1, 8, cz), f32),
-            pltpu.VMEM((shares, 2, 8, cz), f32),
+            pltpu.VMEM((shares, 4, 8, cz), f32),
+            pltpu.VMEM((shares, 18, 8, cz), f32),
             pltpu.SemaphoreType.DMA((flows, 6)),
             pltpu.SemaphoreType.DMA((flows, 6)),
-            pltpu.SemaphoreType.DMA((shares, 6)),
-            pltpu.SemaphoreType.DMA((shares, 6)),
+            pltpu.SemaphoreType.DMA((shares, 27)),
+            pltpu.SemaphoreType.DMA((shares, 27)),
         ],
         compiler_params=pltpu.CompilerParams(collective_id=0, has_side_effects=True),
     )(

time: 112 us -> 86.9 us (0.78)
  Pallas kernels: 91.4 us -> 66 us
    pallas_call x1, Pallas kernels: 91.4 us -> 66 us  [per_device(): pl.pallas_call(functools.partial(kernel, axes), out_shape=(jax.ShapeDtype...]
where the time goes in v2:
time: 86.9 us; the launch traced here: 86.5 us
  Pallas kernels  66 us (76%)
  local copies, waits for them, and re-layouts  10.6 us (12%)
  starting transfers between devices  4.26 us (5%)
  waiting for transfers between devices  3.61 us (4%)
  matrix products  0.87 us (1%)
    pallas_call x1, Pallas kernels, per_device(): pl.pallas_call(functools.partial(kernel, axes), out_shape=(jax.ShapeDtype...  66 us
    unnamed x18, local copies, waits for them, and re-layouts  5.57 us
    all_to_all x1, starting transfers between devices, brick_blocks(): lax.all_to_all(held_blocks, 'gx', split_axis=0, concat_axis=0, tiled=True)  4.26 us
    all_to_all x1, waiting for transfers between devices, brick_blocks(): lax.all_to_all(held_blocks, 'gx', split_axis=0, concat_axis=0, tiled=True)  3.61 us
  transfers between devices with their start and end apart: 1, of which 1 were waited for; matrix products, arithmetic and copies ran while one was open for 1% of the time, Pallas kernels for 0%

profile of v2, /device:TPU:0, one launch (start us, length us, event | category | flops | bytes accessed | tf_op | source)
XLA Modules:
  0.0 86.5 jit_solution(4149528535246620171)
XLA Ops:
  0.6 0.0 copy-start
  0.7 0.9 %copy-done = bf16[1,1,1,2,64,24,24]{4,6,5,3,2,1,0:T(8,128)(2,1)S(1)} copy-done((bf16[1,1,1,2,64,24,24]{4,6,5,3,2,1,0:T(8,128)(2,1)S(1)}, bf16[1,1,1,2,64,24,24]{4,6,5,3,2,1,0:T(8,128)(2,1)}, u32[]{:S(2)}) %copy-start) | copy-done | bytes 147480
  1.6 0.9 %reshape.70 = bf16[2,2,18432]{2,1,0:T(2,128)(2,1)} reshape(bf16[2,24,24,64]{3,2,1,0:T(8,128)(2,1)S(1)} %bitcast_bitcast_fusion) | data formatting | bytes 294912
  2.6 4.3 %all-to-all-start = ((bf16[2,2,18432]{2,1,0:T(2,128)(2,1)}), bf16[2,2,18432]{2,1,0:T(2,128)(2,1)S(1)}, u32[]{:S(2)}, u32[]{:S(2)}) async-start(bf16[2,2,18432]{2,1,0:T(2,128)(2,1)} %reshape.70), calls=%async_computation | async-start | bytes 294912 | tf_op jit(solution)/shard_map/all_to_all | solution.py:41
  6.8 0.7 copy.28.table_ref
  7.5 0.1 fusion.4
  7.6 0.1 reduce_window_sum.11
  7.7 0.2 select_reduce_fusion
  7.9 3.6 %all-to-all-done = bf16[2,2,18432]{2,1,0:T(2,128)(2,1)S(1)} async-done(((bf16[2,2,18432]{2,1,0:T(2,128)(2,1)}), bf16[2,2,18432]{2,1,0:T(2,128)(2,1)S(1)}, u32[]{:S(2)}, u32[]{:S(2)}) %all-to-all-start) | async-done | bytes 147488 | tf_op jit(solution)/shard_map/all_to_all | solution.py:41
  11.5 0.2 reshape.71
  11.7 0.4 copy.32
  12.2 0.0 copy-start.1
  12.2 0.0 copy-start.2
  12.2 0.7 gather_fusion
  12.9 0.8 copy.25
  13.7 0.7 fusion
  14.4 0.0 copy-start.3
  14.4 1.1 %copy.24 = bf16[8,4,8,8,144]{4,3,2,1,0:T(8,128)(2,1)} copy(bf16[8,4,8,8,144]{4,3,1,2,0:T(8,128)(2,1)S(1)} %fusion) | data formatting | bytes 1179648 | tf_op jit(solution)/shard_map/convert_element_type | solution.py:530
  15.5 0.7 gather_fusion.1
  16.2 0.2 fusion.2
  16.4 1.4 %broadcast_in_dim.6.diag_ref = f32[8,8,4,8,128]{4,3,2,1,0:T(8,128)} broadcast(f32[8,8,4,8]{3,2,1,0:T(4,128)S(1)} %copy.27), dimensions={0,1,2,3} | broadcast | bytes 1056768 | tf_op jit(solution)/shard_map/broadcast_in_dim | solution.py:538
  17.8 66.0 %shard_map.131 = (f32[8,8,128]{2,1,0:T(8,128)}, f32[8,8,128]{2,1,0:T(8,128)}) custom-call(f32[5,4]{1,0:T(8,128)} %copy.28.table_ref, s32[64]{0:T(128)} %cells_ref.1, f32[64]{0:T(128)} %rates_ref.1, f32[8,8,128]{2,1,0:T(8,128)} %p0_ref.1, f32[8,8,128]{2,1,0:T(8,128)} %sat_ref.1, f32[8,8,128]{2,1,0:T(8,128)} %perm_ref.1, s32[8,8,128]{2,1,0:T(8,128)} %rock_ref.1, ...), custom_call_target="tpu_custom_call" | custom-call | tf_op jit(solution)/shard_map/pallas_call | solution.py:547
  83.8 1.4 %copy.40 = f32[8,8,128]{2,1,0:T(8,128)} copy(f32[8,8,128]{2,1,0:T(8,128)} %get-tuple-element.4) | data formatting | bytes 65536
  85.1 1.4 %copy.41 = f32[8,8,128]{2,1,0:T(8,128)} copy(f32[8,8,128]{2,1,0:T(8,128)} %get-tuple-element.5) | data formatting | bytes 65536
  (12 shorter events, 0.1 us)
Async XLA Ops:
  0.6 1.0 %copy-start = (bf16[1,1,1,2,64,24,24]{4,6,5,3,2,1,0:T(8,128)(2,1)S(1)}, bf16[1,1,1,2,64,24,24]{4,6,5,3,2,1,0:T(8,128)(2,1)}, u32[]{:S(2)}) copy-start(bf16[1,1,1,2,64,24,24]{4,6,5,3,2,1,0:T(8,128)(2,1)} %param.20) | copy-start | bytes 442372
  0.6 6.2 %copy-start.5 = (f32[5,4]{0,1:T(4,128)S(1)}, f32[5,4]{0,1:T(4,128)}, u32[]{:S(2)}) copy-start(f32[5,4]{0,1:T(4,128)} %param.16) | copy-start | bytes 244
  0.7 6.8 %copy-start.4 = (s32[1,1,1,64,1]{3,4,2,1,0:T(1,128)S(1)}, s32[1,1,1,64,1]{3,4,2,1,0:T(1,128)}, u32[]{:S(2)}) copy-start(s32[1,1,1,64,1]{3,4,2,1,0:T(1,128)} %param.19) | copy-start | bytes 772
  2.6 8.9 %all-to-all-start = ((bf16[2,2,18432]{2,1,0:T(2,128)(2,1)}), bf16[2,2,18432]{2,1,0:T(2,128)(2,1)S(1)}, u32[]{:S(2)}, u32[]{:S(2)}) async-start(bf16[2,2,18432]{2,1,0:T(2,128)(2,1)} %reshape.70), calls=%async_computation | async-start | bytes 294912 | tf_op jit(solution)/shard_map/all_to_all | solution.py:41
  12.2 1.5 %copy-start.1 = (bf16[8,24,144,1]{2,1,0,3:T(8,128)(2,1)S(1)}, bf16[8,24,144,1]{2,1,0,3:T(8,128)(2,1)}, u32[]{:S(2)}) copy-start(bf16[8,24,144,1]{2,1,0,3:T(8,128)(2,1)} %constant.37) | copy-start | bytes 165892
  12.2 1.5 %copy-start.2 = (bf16[4,8,24,1,1]{2,1,0,4,3:T(8,128)(2,1)S(1)}, bf16[4,8,24,1,1]{2,1,0,4,3:T(8,128)(2,1)}, u32[]{:S(2)}) copy-start(bf16[4,8,24,1,1]{2,1,0,4,3:T(8,128)(2,1)} %constant.38) | copy-start | bytes 4612
  14.4 1.8 %copy-start.3 = (bf16[4,8,24,1]{2,1,0,3:T(8,128)(2,1)S(1)}, bf16[4,8,24,1]{2,1,0,3:T(8,128)(2,1)}, u32[]{:S(2)}) copy-start(bf16[4,8,24,1]{2,1,0,3:T(8,128)(2,1)} %constant.39) | copy-start | bytes 4612

commit v3 on v2

--- a/solution.py
+++ b/solution.py
@@ -53,9 +53,9 @@
     rock_ref,
     anch_ref,
     big_ref,
-    diag_ref,
     p_out,
     s_out,
+    diag_ref,
     p,
     cond,
     base,
@@ -134,7 +134,8 @@
     )
 
     def members(group):
-        return [(sx,) + group for sx in (-1, 0, 1) if (sx,) + group != (0, 0, 0)]
+        sides = (-1, 0) if group[1] and count_x == 2 else (-1, 0, 1)
+        return [(sx,) + group for sx in sides if (sx,) + group != (0, 0, 0)]
 
     def guarded(test, act):
         if test is None:
@@ -176,7 +177,8 @@
     def span(axis):
         return 1 + has[axis, 0].astype(jnp.int32) + has[axis, 1].astype(jnp.int32)
 
-    pl.semaphore_wait(barrier, 3 * span("gy") * span("grp") - 1)
+    wide = 2 if count_x == 2 else 3
+    pl.semaphore_wait(barrier, span("gy") * (3 + wide * (span("grp") - 1)) - 1)
 
     lane2 = lax.broadcasted_iota(jnp.int32, (cy, cz), 1)
 
@@ -356,8 +358,8 @@
 
     def share_arrive(slot):
         def arrive(group):
-            for sx, sy, sz in members(group):
-                message(slot, (-sx, -sy, -sz)).wait_recv()
+            for shift in members((-group[0], -group[1])):
+                message(slot, shift).wait_recv()
 
         for group, test in groups.items():
             guarded(test, lambda group=group: arrive(group))
@@ -366,7 +368,7 @@
             total = jnp.zeros((8, cz), jnp.float32)
             for sx in (-1, 0, 1):
                 for sy in (-1, 0, 1):
-                    part = nz_recv[slot, z_place(sx, sy, sz)]
+                    part = nz_recv[slot, z_place(abs(sx) if count_x == 2 else sx, sy, sz)]
                     turn = (sx * cx * (cy + 1) + sy * cy) % cz
                     part = pltpu.roll(part, turn, 1) if turn else part
                     for test in (line_x[sx], line_y[sy]):
@@ -398,6 +400,16 @@
         for group, test in groups.items():
             guarded(test, lambda group=group: sent(group))
 
+    rows = cy * 8
+    offset = lax.broadcasted_iota(jnp.int32, (rows, big_ref.shape[2]), 1) - (
+        lax.broadcasted_iota(jnp.int32, (rows, big_ref.shape[2]), 0)
+    )
+    for i in range(cx):
+        for q in range(4):
+            block = big_ref[i, q * rows : (q + 1) * rows, :].astype(jnp.float32)
+            on = offset == (q // 2) * (cy + 1) * 8 + (q % 2) * 8
+            entry = jnp.sum(jnp.where(on, block, 0.0), axis=1, keepdims=True)
+            diag_ref[i, q] = jnp.broadcast_to(entry, (rows, cz)).reshape(cy, 8, cz)
     for x in range(cx + 1):
         for y in range(cy + 1):
             total = jnp.zeros((8, cz), jnp.float32)
@@ -408,7 +420,7 @@
                         held = jnp.broadcast_to(
                             anch_ref[i, k : k + 1, :].astype(jnp.float32), (8, cz)
                         )
-                        total = total + jnp.where(comp == 3, held, diag_ref[i, k, 2 * dx + dy])
+                        total = total + jnp.where(comp == 3, held, diag_ref[i, 2 * dx + dy, k])
             res[x, y] = total
     share_start(0)
     disp[...] = jnp.zeros_like(disp)
@@ -504,6 +516,11 @@
     s_out[...] = strain[...]
 
 
+def hand_on(p_ref, s_ref, p_out, s_out):
+    p_out[...] = p_ref[...]
+    s_out[...] = s_ref[...]
+
+
 def per_device(
     pressure_start,
     saturation,
@@ -529,13 +546,6 @@
         "qmr,ikrc->iqkmc", rows_b, spread, preferred_element_type=jnp.float32
     ).astype(jnp.bfloat16)
     big = big.reshape(cx, 4 * cy * 8, cols.shape[2])
-    diag = jnp.einsum(
-        "qmr,ikr->ikqm",
-        rows_b,
-        jnp.diagonal(shaped, axis1=2, axis2=3),
-        preferred_element_type=jnp.float32,
-    )
-    diag = jnp.broadcast_to(diag[..., None], (cx, cy, 4, 8, cz))
 
     cell = (cx, cy, cz)
     line = (cx + 1, cy + 1, 8, cz)
@@ -544,12 +554,13 @@
     f32 = jnp.float32
     vmem = pl.BlockSpec(memory_space=pltpu.VMEM)
     smem = pl.BlockSpec(memory_space=pltpu.SMEM)
-    return pl.pallas_call(
+    held = pl.pallas_call(
         functools.partial(kernel, axes),
         out_shape=(jax.ShapeDtypeStruct(cell, f32), jax.ShapeDtypeStruct(cell, f32)),
-        in_specs=[smem] * 3 + [vmem] * 7,
+        in_specs=[smem] * 3 + [vmem] * 6,
         out_specs=(vmem, vmem),
-        scratch_shapes=[pltpu.VMEM(cell, f32)] * 7
+        scratch_shapes=[pltpu.VMEM((cx, 4, cy, 8, cz), f32)]
+        + [pltpu.VMEM(cell, f32)] * 7
         + [pltpu.VMEM((6,) + cell, f32)]
         + [pltpu.VMEM(cell, f32)] * 2
         + [pltpu.VMEM(line, f32)] * 5
@@ -580,8 +591,13 @@
         rock_type,
         anchored,
         big,
-        diag,
-    )
+    )
+    return pl.pallas_call(
+        hand_on,
+        out_shape=(jax.ShapeDtypeStruct(cell, f32), jax.ShapeDtypeStruct(cell, f32)),
+        in_specs=[vmem] * 2,
+        out_specs=(vmem, vmem),
+    )(*held)
 
 
 def solution(mesh):

time: 86.9 us -> 80.2 us (0.923)
  local copies, waits for them, and re-layouts: 10.6 us -> 4.99 us
    unnamed x18 -> x14, local copies, waits for them, and re-layouts: 5.57 us -> 2.8 us
    pallas_call x1, Pallas kernels: 66 us -> 63.9 us  [per_device(): pl.pallas_call(functools.partial(kernel, axes), out_shape=(jax.ShapeDtype...]
    pallas_call x0 -> x1, Pallas kernels: none -> 1.4 us  [per_device(): pl.pallas_call(hand_on, out_shape=(jax.ShapeDtypeStruct(cell, f32), jax.S...]
    broadcast_in_dim x1 -> x0, local copies, waits for them, and re-layouts: 1.35 us -> none  [per_device(): diag = jnp.broadcast_to(diag[..., None], (cx, cy, 4, 8, cz))]
where the time goes in v3:
time: 80.2 us; the launch traced here: 79.9 us
  Pallas kernels  65.3 us (81%)
  local copies, waits for them, and re-layouts  4.99 us (6%)
  starting transfers between devices  4.26 us (5%)
  waiting for transfers between devices  3.62 us (5%)
    pallas_call x1, Pallas kernels, per_device(): pl.pallas_call(functools.partial(kernel, axes), out_shape=(jax.ShapeDtype...  63.9 us
    all_to_all x1, starting transfers between devices, brick_blocks(): lax.all_to_all(held_blocks, 'gx', split_axis=0, concat_axis=0, tiled=True)  4.26 us
    all_to_all x1, waiting for transfers between devices, brick_blocks(): lax.all_to_all(held_blocks, 'gx', split_axis=0, concat_axis=0, tiled=True)  3.62 us
    unnamed x14, local copies, waits for them, and re-layouts  2.8 us
  transfers between devices with their start and end apart: 1, of which 1 were waited for; matrix products, arithmetic and copies ran while one was open for 1% of the time, Pallas kernels for 0%

profile of v3, /device:TPU:0, one launch (start us, length us, event | category | flops | bytes accessed | tf_op | source)
XLA Modules:
  0.0 79.9 jit_solution(18196152600931180882)
XLA Ops:
  0.6 0.0 copy-start
  0.6 0.0 copy-start.3
  0.7 0.0 copy-start.4
  0.7 0.9 %copy-done = bf16[1,1,1,2,64,24,24]{4,6,5,3,2,1,0:T(8,128)(2,1)S(1)} copy-done((bf16[1,1,1,2,64,24,24]{4,6,5,3,2,1,0:T(8,128)(2,1)S(1)}, bf16[1,1,1,2,64,24,24]{4,6,5,3,2,1,0:T(8,128)(2,1)}, u32[]{:S(2)}) %copy-start) | copy-done | bytes 147480
  1.6 0.9 %reshape.61 = bf16[2,2,18432]{2,1,0:T(2,128)(2,1)} reshape(bf16[2,24,24,64]{3,2,1,0:T(8,128)(2,1)S(1)} %bitcast_bitcast_fusion) | data formatting | bytes 294912
  2.5 4.3 %all-to-all-start = ((bf16[2,2,18432]{2,1,0:T(2,128)(2,1)}), bf16[2,2,18432]{2,1,0:T(2,128)(2,1)S(1)}, u32[]{:S(2)}, u32[]{:S(2)}) async-start(bf16[2,2,18432]{2,1,0:T(2,128)(2,1)} %reshape.61), calls=%async_computation | async-start | bytes 294912 | tf_op jit(solution)/shard_map/all_to_all | solution.py:41
  6.8 0.0 copy-done.3
  6.8 0.1 fusion.2
  6.9 0.1 reduce_window_sum.11
  7.0 0.2 select_reduce_fusion
  7.2 0.0 copy-done.4
  7.2 0.7 copy.22.table_ref
  7.9 0.0 copy-start.1
  7.9 0.0 copy-start.2
  7.9 3.6 %all-to-all-done = bf16[2,2,18432]{2,1,0:T(2,128)(2,1)S(1)} async-done(((bf16[2,2,18432]{2,1,0:T(2,128)(2,1)}), bf16[2,2,18432]{2,1,0:T(2,128)(2,1)S(1)}, u32[]{:S(2)}, u32[]{:S(2)}) %all-to-all-start) | async-done | bytes 147488 | tf_op jit(solution)/shard_map/all_to_all | solution.py:41
  11.5 0.2 reshape.62
  11.7 0.4 copy.25
  12.2 0.7 gather_fusion
  12.8 0.0 copy-done.1
  12.8 0.0 copy-done.2
  12.8 0.7 fusion
  13.5 1.1 %copy.21 = bf16[8,4,8,8,144]{4,3,2,1,0:T(8,128)(2,1)} copy(bf16[8,4,8,8,144]{4,3,1,2,0:T(8,128)(2,1)S(1)} %fusion) | data formatting | bytes 1179648 | tf_op jit(solution)/shard_map/convert_element_type | solution.py:547
  14.6 63.9 %shard_map.131 = (f32[8,8,128]{2,1,0:T(8,128)}, f32[8,8,128]{2,1,0:T(8,128)}) custom-call(f32[5,4]{1,0:T(8,128)} %copy.22.table_ref, s32[64]{0:T(128)} %cells_ref.1, f32[64]{0:T(128)} %rates_ref.1, f32[8,8,128]{2,1,0:T(8,128)} %p0_ref.1, f32[8,8,128]{2,1,0:T(8,128)} %sat_ref.1, f32[8,8,128]{2,1,0:T(8,128)} %perm_ref.1, s32[8,8,128]{2,1,0:T(8,128)} %rock_ref.1, ...), custom_call_target="tpu_custom_call" | custom-call | tf_op jit(solution)/shard_map/pallas_call | solution.py:557
  78.5 1.4 %shard_map.132 = (f32[8,8,128]{2,1,0:T(8,128)}, f32[8,8,128]{2,1,0:T(8,128)}) custom-call(f32[8,8,128]{2,1,0:T(8,128)} %get-tuple-element.4.p_ref, f32[8,8,128]{2,1,0:T(8,128)} %get-tuple-element.5.s_ref), custom_call_target="tpu_custom_call" | custom-call | tf_op jit(solution)/shard_map/pallas_call | solution.py:595
  (3 shorter events, 0.0 us)
Async XLA Ops:
  0.6 1.0 %copy-start = (bf16[1,1,1,2,64,24,24]{4,6,5,3,2,1,0:T(8,128)(2,1)S(1)}, bf16[1,1,1,2,64,24,24]{4,6,5,3,2,1,0:T(8,128)(2,1)}, u32[]{:S(2)}) copy-start(bf16[1,1,1,2,64,24,24]{4,6,5,3,2,1,0:T(8,128)(2,1)} %param.20) | copy-start | bytes 442372
  0.6 6.2 %copy-start.3 = (s32[1,1,1,64,1]{3,4,2,1,0:T(1,128)S(1)}, s32[1,1,1,64,1]{3,4,2,1,0:T(1,128)}, u32[]{:S(2)}) copy-start(s32[1,1,1,64,1]{3,4,2,1,0:T(1,128)} %param.19) | copy-start | bytes 772
  0.7 6.5 %copy-start.4 = (f32[5,4]{0,1:T(4,128)S(1)}, f32[5,4]{0,1:T(4,128)}, u32[]{:S(2)}) copy-start(f32[5,4]{0,1:T(4,128)} %param.16) | copy-start | bytes 244
  2.5 8.9 %all-to-all-start = ((bf16[2,2,18432]{2,1,0:T(2,128)(2,1)}), bf16[2,2,18432]{2,1,0:T(2,128)(2,1)S(1)}, u32[]{:S(2)}, u32[]{:S(2)}) async-start(bf16[2,2,18432]{2,1,0:T(2,128)(2,1)} %reshape.61), calls=%async_computation | async-start | bytes 294912 | tf_op jit(solution)/shard_map/all_to_all | solution.py:41
  7.9 5.0 %copy-start.1 = (bf16[8,24,144,1]{2,1,0,3:T(8,128)(2,1)S(1)}, bf16[8,24,144,1]{2,1,0,3:T(8,128)(2,1)}, u32[]{:S(2)}) copy-start(bf16[8,24,144,1]{2,1,0,3:T(8,128)(2,1)} %constant.19) | copy-start | bytes 165892
  7.9 5.0 %copy-start.2 = (bf16[4,8,24,1,1]{2,1,0,4,3:T(8,128)(2,1)S(1)}, bf16[4,8,24,1,1]{2,1,0,4,3:T(8,128)(2,1)}, u32[]{:S(2)}) copy-start(bf16[4,8,24,1,1]{2,1,0,4,3:T(8,128)(2,1)} %constant.20) | copy-start | bytes 4612
